TPU v7x, 32 devices: a whole 2x2x4 slice. The times are simulated.
32 devices in a mesh: dp: 8 (over z, x), head: 4 (over y, core).
Axes of the slice: x: 2, y: 2, z: 4, core: 2. Of those that a mesh axis runs over, the one named last changes fastest.
Arguments:
- layer_input: bfloat16 [64, 197, 768], P(('dp', 'head')), may hold values from -6 to 6
- prompts: bfloat16 [100, 768], replicated, may hold values from -6 to 6
- lengths: int32 [64], P('dp'), may hold values from 1 to 100, as said below
- key_mask: int32 [64, 297], P('dp'), may hold values 0 or 1
- ln1_gain: float32 [768], replicated, may hold values from 0.1 to 1.9
- ln1_shift: float32 [768], replicated, may hold values from -1.5 to 1.5
- w_qkv: bfloat16 [3, 768, 768], P(None, 'dp', 'head'), may hold values from -0.3125 to 0.3125
- w_out: bfloat16 [768, 768], P('head', 'dp'), may hold values from -0.875 to 0.875
- b_out: float32 [768], replicated, may hold values from -1.5 to 1.5
- ln2_gain: float32 [768], replicated, may hold values from 0.1 to 1.9
- ln2_shift: float32 [768], replicated, may hold values from -1.5 to 1.5
- w_fc1: bfloat16 [768, 3072], P('dp', 'head'), may hold values from -0.21875 to 0.21875
- b_fc1: float32 [3072], P('head'), may hold values from -2.5 to 2.5
- w_fc2: bfloat16 [3072, 768], P('head', 'dp'), may hold values from -0.15625 to 0.15625
- b_fc2: float32 [768], replicated, may hold values from -1.5 to 1.5
- grad_output: bfloat16 [64, 297, 768], P(('dp', 'head')), may hold values from -6 to 6
Outputs:
- layer_output: bfloat16 [64, 297, 768], P(('dp', 'head'))
- grad_input: bfloat16 [64, 197, 768], P(('dp', 'head'))
- grad_prompts: float32 [100, 768], replicated
Inputs may be any that keep to these rules, and one draw needn't show every extreme that they name: `lengths`: each length is one of 1, 10, 50 and 100; both 1 and 100 occur.
All inputs are finite; a program needn't handle non-finite values. No bound on the sum of `key_mask` on one device may be relied on, other than what follows from the above.
Results may differ from a plain program's by a relative error of at most 0.019.
Values may be sent and summed in bfloat16 or wider, within the bound.
No kernel may reach another device: no remote copies, remote signals or barrier semaphores. Data moves between devices by JAX's collectives and lax.ppermute only.
A program may use at most 128 MiB of HBM per device.

v0:
```python
import functools

import jax
import jax.numpy as jnp
from jax import lax
from jax.experimental import pallas as pl
from jax.experimental.pallas import tpu as pltpu
from jax.sharding import PartitionSpec as P

HEAD_DIM = 64
IMG_TOK = 197
PROMPTS = 100
SEQ = IMG_TOK + PROMPTS
ROWS = 304
KEYS = 384
EPSILON = 1e-06
GRANTS = (9, 9, 9, 11)
COST_SCALE = 10.0
CHUNKS = (256, 256, 256)
BOTH = ("dp", "head")
F32 = jnp.float32
BF16 = jnp.bfloat16

NN = (((1,), (0,)), ((), ()))
NT = (((1,), (1,)), ((), ()))
TN = (((0,), (0,)), ((), ()))


def dot(left, right, dims):
    return lax.dot_general(left, right, dims, preferred_element_type=F32)


def device_perm(count, target):
    pairs = []
    for index in range(count):
        c, y, x, z = index % 2, index // 2 % 2, index // 4 % 2, index // 8
        z, x, y, c = target(z, x, y, c)
        pairs.append((index, ((z * 2 + x) * 2 + y) * 2 + c))
    return pairs


def along_ring(z, step, depth):
    place = ((z ^ (z >> 1)) + step + depth) % depth
    return place ^ (place >> 1)


class Exchange:
    def __init__(self, dp, head):
        self.count = dp * head
        self.depth = dp // 2

    def move(self, value, target):
        return lax.ppermute(value, BOTH, device_perm(self.count, target))

    def from_z(self, value, step):
        return self.move(value, lambda z, x, y, c: (along_ring(z, -step, self.depth), x, y, c))

    def first(self, value):
        return self.move(value, lambda z, x, y, c: (z, x ^ (1 - c), y ^ c, c))

    def second(self, value):
        return self.move(value, lambda z, x, y, c: (z, x ^ c, y ^ (1 - c), c))

    def core(self, value):
        return self.move(value, lambda z, x, y, c: (z, x, y, 1 - c))

    def swap(self, value, dz=0, dx=0, dy=0):
        return self.move(value, lambda z, x, y, c: (z ^ dz, x ^ dx, y ^ dy, c))


def tie(*values):
    return lax.optimization_barrier(values)


ALL, UP, DOWN = range(3)
NEAR_FAR = ((0, 0), (1, 0), (0, 1), (1, 1))


class Held:
    def __init__(self, exchange):
        self.exchange = exchange
        self.arrays, self.plan = [], []

    def add(self, array, lane, steps, halves, is_other=0, kind=ALL):
        self.arrays.append(array)
        entries = [(step, half, is_far, is_other) for half, is_far in halves for step in steps]
        self.plan.append((lane, kind, entries))

    def add_both(self, array, steps, halves):
        self.add(array, 0, steps, halves, 0)
        self.add(self.exchange.core(array), 0, steps, halves, 1)

    def add_pair(self, pair, lane, steps, halves, kind=ALL):
        for is_other, array in enumerate(pair):
            self.add(array, lane, steps, halves, is_other, kind)


class Gather:
    def __init__(self, exchange, own, both, later, bias):
        self.exchange, self.width, self.part = exchange, own.shape[1], later.shape[1] // 2
        own, both, self.later, self.bias = own[None], both[None], later[None], bias
        first = exchange.first(both)
        self.came = jnp.concatenate([exchange.from_z(own, 1), exchange.from_z(own, 3)])
        self.own = both, first

    def attention(self, *ready):
        exchange, width, part = self.exchange, self.width, self.part
        both, first, came, later, bias = tie(*self.own, self.came, self.later, self.bias)
        near = jnp.concatenate([both, first])
        own_far = exchange.second(near)
        two = exchange.from_z(came[:1], 1)
        other = exchange.core(bias)
        at_low = lax.axis_index("head") % 2 == 0
        bias = jnp.where(at_low, jnp.stack([bias, other]), jnp.stack([other, bias]))
        own_near, own_far, base, later, bias, *ready = tie(
            near, own_far, jnp.concatenate([came, two]), later, bias, *ready
        )
        first = exchange.first(base)
        later_one = exchange.from_z(later, 1)
        owns = (own_near, own_far, exchange.core(own_near), exchange.core(own_far))
        near, later_one, later, bias, *owns = tie(
            jnp.concatenate([base, first]), later_one, later, bias, *owns
        )
        far = exchange.second(near)
        later_three = exchange.from_z(later, 3)
        later_two = exchange.from_z(later_one, 1)
        other_near = exchange.core(near)
        self.bias = jnp.concatenate([bias, exchange.swap(bias, dy=1)])
        far, base, self.plane, self.bias = tie(
            far,
            jnp.concatenate([later, later_one, later_three, later_two]),
            jnp.concatenate([owns[0][:, :, width:], owns[1][:, :, width:]]),
            self.bias,
        )
        near_later = jnp.concatenate([base, exchange.first(base)])
        self.up = exchange.from_z(self.plane, 1)
        self.later_near, self.up, self.plane = tie(near_later, self.up, self.plane)
        self.split = part + part // 2
        self.later_far = exchange.second(self.later_near[:, :, : self.split])
        self.other_near = exchange.core(self.later_near)
        self.down = exchange.from_z(self.plane, 3)
        self.low = exchange.from_z(self.up[:2], 1)

        held = Held(exchange)
        self.parts = [Held(exchange) for _ in range(3)]
        for index, array in enumerate(owns):
            halves = NEAR_FAR[2 * (index % 2) : 2 * (index % 2) + 2]
            held.add(array, 0, (0,), halves, index // 2)
            self.parts[1].add(array, width, (0,), halves, index // 2)
        held.add(near, 0, (1, 3, 2), NEAR_FAR[:2], 0)
        held.add(other_near, 0, (1, 3, 2), NEAR_FAR[:2], 1)
        held.add_both(far, (1, 3, 2), NEAR_FAR[2:])
        return held, ready

    def round_seven(self, token):
        exchange, steps = self.exchange, (0, 1, 3, 2)
        near, far, up, down, low, token = tie(
            self.later_near, self.later_far, self.up, self.down, self.low, token
        )
        self.rest = exchange.second(near[:, :, self.split :])
        self.high = exchange.from_z(down[2:], 3)
        near, far = (near, self.other_near), (far, exchange.core(far))
        self.parts[2].add_pair(near, self.part, steps, NEAR_FAR[:2])
        self.parts[2].add_pair(far, self.part, steps, NEAR_FAR[2:], UP)
        self.halves = [Held(exchange), Held(exchange)]
        for is_other, held in enumerate(self.halves):
            held.add(near[is_other], 0, steps, NEAR_FAR[:2], is_other)
            held.add(far[is_other], 0, steps, NEAR_FAR[2:], is_other)
        self.parts[1].add_both(up, (1,), NEAR_FAR)
        self.parts[1].add_both(down, (3,), NEAR_FAR)
        self.parts[1].add_both(low, (2,), NEAR_FAR[:2])
        return token

    def round_eight(self, token):
        high, rest, token = tie(self.high, self.rest, token)
        self.parts[1].add_both(high, (2,), NEAR_FAR[2:])
        self.parts[2].add_pair((rest, self.exchange.core(rest)), 0, (0, 1, 3, 2), NEAR_FAR[2:], DOWN)
        return token


def placement(entry, place, depth):
    z, x, y, c = place
    step, half, is_far, is_other = entry
    core = 1 - c if is_other else c
    dx = jnp.where(core == 0, half, is_far)
    dy = jnp.where(core == 0, is_far, half)
    block = along_ring(z, step, depth) * 2 + jnp.where(dx == 1, 1 - x, x)
    return block, dy, core


def row_mean(value):
    return jnp.mean(value, axis=-1, keepdims=True)


def normalized(rows):
    center = rows - row_mean(rows)
    scale = lax.rsqrt(row_mean(center * center) + EPSILON)
    return center * scale, scale


def norm_back(grad, gain, unit, scale):
    grad = grad * gain
    return scale * (grad - row_mean(grad) - unit * row_mean(grad * unit))


def low_lanes(rows):
    return lax.broadcasted_iota(jnp.int32, (rows, 128), 1) < HEAD_DIM


def both_halves(tile, keep):
    zero = jnp.zeros_like(tile)
    return jnp.concatenate([jnp.where(keep, tile, zero), jnp.where(keep, zero, tile)], axis=0)


def side_to_rows(pair):
    return jnp.concatenate([pair[:, :KEYS], pair[:, KEYS:]], axis=0)


def by_blocks(rows, size, body):
    @pl.loop(0, rows // size)
    def _(index):
        body(pl.ds(pl.multiple_of(index * size, size), size))


class Loader:
    def __init__(self, plan, depth):
        self.plan, self.depth = plan, depth
        self.count = len(plan)

    def run(self, place_ref, pieces, put):
        place = tuple(place_ref[i] for i in range(4))
        for ref, (lane, kind, entries) in zip(pieces, self.plan):
            for index, entry in enumerate(entries):
                rows = ref.shape[1]
                if self.depth:
                    block, dy, core = placement(entry, place, self.depth)
                    where = pl.ds(pl.multiple_of(block * rows, rows), rows)
                else:
                    (dy, core), where = entry, pl.ds(0, rows)
                put(ref.at[index, :, lane:], where, dy, core, kind)


def lanes_at(start, size):
    return pl.ds(pl.multiple_of(start, 128), size)


def put_attn(wide, out, raw):
    def put(source, rows, dy, core, kind):
        slot = dy * 2 + core
        wide[dy, rows, lanes_at(core * 384, 384)] = source[:, :384]
        out[rows, lanes_at(slot * 128, 128)] = source[:, 384:512]
        raw[rows, lanes_at(slot * 256, 256)] = source[:, 512:768]

    return put


def join_thirds(raw, dy, wide, out):
    even, odd = raw[:, dy * 512 : dy * 512 + 256], raw[:, dy * 512 + 256 : dy * 512 + 512]
    low = low_lanes(even.shape[0])
    at = dy * 384
    wide[:, at : at + 128] = jnp.where(low, even[:, :128], odd[:, :128])
    wide[:, at + 128 : at + 256] = jnp.where(low, even[:, 128:], odd[:, 128:])
    wide[:, at + 256 : at + 384] = jnp.where(low, odd[:, :128], even[:, :128])
    out[:, dy * 128 : dy * 128 + 128] = jnp.where(low, odd[:, 128:], even[:, 128:])


def put_mlp(up, down, chunk, slots):
    def put(source, rows, dy, core, kind):
        lanes = lanes_at((dy if slots == 2 else dy * 2 + core) * chunk, chunk)
        if kind != DOWN:
            up[rows, lanes] = source[:, :chunk]
        if kind != UP:
            start = 0 if kind == DOWN else chunk
            down[rows, lanes] = source[:, start : start + chunk]

    return put


def attend_units(images, pair, normed, weights, visible, qkv_out, exps_out, ctx_out, inv_out):
    qkv = dot(normed[...], weights, NN)
    low = low_lanes(KEYS)
    keep = jnp.logical_xor(low, pair == 2)
    counts = both_halves(jnp.ones((KEYS, 128), BF16), keep)
    padding = jnp.zeros((KEYS - ROWS, 128), BF16)
    for image in range(images):
        rows = slice(image * ROWS, (image + 1) * ROWS)
        see = visible[image] > 0
        for unit in range(2):
            tiles = [qkv[rows, unit * 384 + at : unit * 384 + at + 128] for at in (0, 128, 256)]
            query = (tiles[0] * 0.125).astype(BF16)
            key, value = (
                jnp.concatenate([tile.astype(BF16), padding], axis=0) for tile in tiles[1:]
            )
            qkv_out[pair, unit, image, :ROWS, :128] = query
            qkv_out[pair, unit, image, :, 128:256] = key
            qkv_out[pair, unit, image, :, 256:] = value
            scores = dot(query, both_halves(key, low), NT)
            parts = []
            for head in range(2):
                part = jnp.where(see, scores[:, head * KEYS : (head + 1) * KEYS], -1000000000.0)
                part = jnp.exp(part - jnp.max(part, axis=-1, keepdims=True))
                parts.append(part.astype(BF16))
            exps = jnp.concatenate(parts, axis=1)
            exps_out[pair, unit, image] = exps
            mixed = dot(exps, jnp.concatenate([both_halves(value, keep), counts], axis=1), NN)
            inverse = 1.0 / mixed[:, 128:]
            at = slice(unit * 128, unit * 128 + 128)
            inv_out[pair, rows, at] = inverse
            ctx_out[pair, rows, at] = (mixed[:, :128] * inverse).astype(BF16)


def pack_kernel(chunks, place, w_qkv, w_out, w_fc1, fc2_t, own, both, later, qkv, out, sems):
    moves = [(w_qkv, qkv), (w_out, out)]
    start = 0
    for index, chunk in enumerate(chunks):
        target, at = (both, 768) if index == 1 else (later, index * chunk)
        for offset, weight in ((0, w_fc1), (chunk, fc2_t)):
            goal = target.at[:, at + offset : at + offset + chunk]
            moves.append((weight.at[:, start : start + chunk], goal))
        start += chunk
    copies = [
        pltpu.make_async_copy(source, goal, sems.at[index])
        for index, (source, goal) in enumerate(moves)
    ]
    for copy in copies:
        copy.start()
    for copy in copies[:2]:
        copy.wait()
    core = place[3]
    out_t = out[...].T
    for at, value in enumerate((qkv[0], qkv[1], qkv[2], out_t)):
        own[:, at * 128 : at * 128 + 128] = value[:, :128]
    pairs = ((qkv[0][:, 128:], qkv[2][:, 128:]), (qkv[1][:, 128:], out_t[:, 128:]))
    for at, (left, right) in enumerate(pairs):
        straight = jnp.concatenate([left, right], axis=1)
        turned = jnp.concatenate([right, left], axis=1)
        own[:, 512 + at * 128 : 640 + at * 128] = jnp.where(core == 0, straight, turned)
    both[:, :768] = own[...]
    for copy in copies[2:]:
        copy.wait()


def token_kernel(images, *refs):
    place, lengths, tokens, prompts, key_mask, grads, gain, shift = refs[:8]
    stream, normed, grad, visible, rows_f32 = refs[8:]
    position = lax.broadcasted_iota(jnp.int32, (SEQ, 1), 0)
    lane = lax.broadcasted_iota(jnp.int32, (1, SEQ), 1)
    for image in range(images):
        own = place[4] + image
        length = lengths[own]
        base = image * ROWS
        rows_f32[:IMG_TOK] = tokens[image].astype(F32)
        rows_f32[IMG_TOK:SEQ] = prompts[...].astype(F32)
        rows_f32[SEQ:] = jnp.zeros((ROWS - SEQ, rows_f32.shape[1]), F32)
        for start in (0, 152):
            rows = rows_f32[start : start + 152]
            stream[base + start : base + start + 152] = rows.astype(BF16)
            made = normalized(rows)[0] * gain[...] + shift[...]
            normed[base + start : base + start + 152] = made.astype(BF16)
        grad[base + ROWS - 16 : base + ROWS] = jnp.zeros((16, grad.shape[1]), BF16)
        used = position < IMG_TOK + length
        value = grads[image].astype(F32)
        grad[base : base + SEQ] = jnp.where(used, value, 0.0).astype(BF16)
        seen = (key_mask[pl.ds(own, 1)] == 1) | (lane == 0)
        visible[image] = jnp.zeros((1, KEYS), F32)
        visible[image, :, :SEQ] = (seen & (lane < IMG_TOK + length)).astype(F32)


def attend_kernel(loader, images, *refs):
    place, normed, visible, stream, b_out, gain, shift = refs[:7]
    pieces, refs = refs[7 : 7 + loader.count], refs[7 + loader.count :]
    qkv_out, exps_out, ctx_out, inv_out, mid_out, normed_out, wide, out, raw = refs
    loader.run(place, pieces, put_attn(wide, out, raw))
    for dy in range(2):
        join_thirds(raw, dy, wide.at[2], out.at[:, 512:])

    @pl.loop(0, 3)
    def _(pair):
        attend_units(
            images, pair, normed, wide[pair], visible, qkv_out, exps_out, ctx_out, inv_out
        )

    joined = jnp.concatenate([ctx_out[0], ctx_out[1], ctx_out[2]], axis=1)
    mid_out[...] = dot(joined, out[...], NT)

    def finish(rows):
        mid = stream[rows].astype(F32) + mid_out[rows] + b_out[...]
        mid_out[rows] = mid
        normed_out[rows] = (normalized(mid)[0] * gain[...] + shift[...]).astype(BF16)

    by_blocks(images * ROWS, 304, finish)


def gelu_parts(pre):
    density = jnp.exp(pre * pre * -0.5) * 0.3989422804014327
    chance = 0.5 + 0.5 * lax.erf(pre * 0.7071067811865476)
    return chance, density


def mlp_kernel(loader, chunk, slots, first, *refs):
    place, normed, grad, bias = refs[:4]
    refs = refs[4:]
    refs = refs if first else refs[2:]
    pieces = refs[: loader.count]
    out_sum, back_sum, up, down = refs[loader.count :]
    loader.run(place, pieces, put_mlp(up, down, chunk, slots))
    if first:
        out_sum[...] = jnp.zeros_like(out_sum)
        back_sum[...] = jnp.zeros_like(back_sum)
    half = normed.shape[0] // 2
    step = 1024

    @pl.loop(0, up.shape[1] // step)
    def _(index):
        cols = lanes_at(index * step, step)
        for part in range(2):
            rows = slice(part * half, (part + 1) * half)
            pre = dot(normed[rows], up[:, cols], NN) + bias[:, cols]
            grad_active = dot(grad[rows], down[:, cols], NN)
            chance, density = gelu_parts(pre)
            active = (pre * chance).astype(BF16)
            grad_pre = (grad_active * (chance + pre * density)).astype(BF16)
            out_sum[rows] += dot(active, down[:, cols], NT)
            back_sum[rows] += dot(grad_pre, up[:, cols], NT)


LATE = 192


def row_groups(images, late):
    start, stop = (LATE, ROWS) if late else (0, LATE)
    return [slice(image * ROWS + start, image * ROWS + stop) for image in range(images)]


def stream_grad(images, late, stacked, weights, stream, grad_mid, gain, body):
    for image, rows in enumerate(row_groups(images, late)):
        grads = stacked[rows]
        total = dot(grads[:, :768], weights[0], NT) + dot(grads[:, 768:1536], weights[1], NT)
        total = total + dot(grads[:, 1536:], weights[2], NT)
        unit, scale = normalized(stream[rows].astype(F32))
        body(image, grad_mid[rows] + norm_back(total, gain[...], unit, scale))


def back_kernel(images, *refs):
    place, mid, grad_normed, grad, stream, qkv, exps, context, inverse = refs[:9]
    gain_two, gain_one, wide, out = refs[9:13]
    keep_out, give_out, edge, grad_mid, stacked, grad_attn, grad_ctx = refs[13:]

    def begin(rows):
        unit, scale = normalized(mid[rows])
        back = grad[rows].astype(F32) + norm_back(grad_normed[rows], gain_two[...], unit, scale)
        grad_mid[rows] = back
        grad_attn[rows] = back.astype(BF16)

    by_blocks(images * ROWS, 304, begin)
    gradient = dot(grad_attn[...], out[...], NN)
    for index in range(3):
        grad_ctx[index] = gradient[:, index * 256 : index * 256 + 256]

    @pl.loop(0, 3)
    def _(pair):
        low = low_lanes(KEYS)
        keep = jnp.logical_xor(low, pair == 2)
        for image in range(images):
            rows = slice(image * ROWS, (image + 1) * ROWS)
            for unit in range(2):
                at = slice(unit * 128, unit * 128 + 128)
                scaled = (grad_ctx[pair, rows, at] * inverse[pair, rows, at]).astype(BF16)
                product = scaled.astype(F32) * context[pair, rows, at].astype(F32)
                query = qkv[pair, unit, image, :ROWS, :128]
                keys = both_halves(
                    qkv[pair, unit, image, :, 128:256] * jnp.asarray(0.125, BF16), low
                )
                values = both_halves(qkv[pair, unit, image, :, 256:], keep)
                grad_probs = dot(scaled, values, NT)
                parts = []
                for head in range(2):
                    lanes = slice(head * KEYS, (head + 1) * KEYS)
                    own = keep[:ROWS] if head == 0 else jnp.logical_not(keep[:ROWS])
                    delta = jnp.sum(jnp.where(own, product, 0.0), axis=-1, keepdims=True)
                    weight = exps[pair, unit, image, :, lanes].astype(F32)
                    parts.append((weight * (grad_probs[:, lanes] - delta)).astype(BF16))
                grad_scores = jnp.concatenate(parts, axis=1)
                weights = side_to_rows(exps[pair, unit, image])
                made = (
                    dot(grad_scores, keys, NN),
                    dot(side_to_rows(grad_scores), both_halves(query, low[:ROWS]), TN)[:ROWS],
                    dot(weights, both_halves(scaled, keep[:ROWS]), TN)[:ROWS],
                )
                for index, value in enumerate(made):
                    to = lanes_at(pair * 768 + unit * 384 + index * 128, 128)
                    stacked[rows, to] = value.astype(BF16)

    sums = []

    def finish(image, back):
        edge[image] = back[: IMG_TOK - LATE]
        sums.append(back[IMG_TOK - LATE : SEQ - LATE])

    stream_grad(images, True, stacked, wide, stream, grad_mid, gain_one, finish)
    prompt_sum = functools.reduce(jnp.add, sums)
    half = prompt_sum.shape[1] // 2
    low, high = prompt_sum[:, :half], prompt_sum[:, half:]
    keep_low = (place[3] == 0) | (give_out.dtype == F32)
    keep_out[...] = jnp.where(keep_low, low, high)
    give_out[...] = jnp.where(keep_low, high, low).astype(give_out.dtype)


def last_kernel(images, *refs):
    place, lengths, mid, mlp_out, stream, b_fc2, gain_one, wide = refs[:8]
    edge, grad_mid, stacked, result, grad_input = refs[8:]
    width = mid.shape[1]
    position = lax.broadcasted_iota(jnp.int32, (ROWS, 1), 0)
    for image in range(images):
        rows = slice(image * ROWS, (image + 1) * ROWS)
        used = (position < IMG_TOK + lengths[place[4] + image]).astype(F32)
        rows_out = (mid[rows] + mlp_out[rows] + b_fc2[...]) * used
        result[:, image * width : (image + 1) * width] = rows_out[:SEQ].astype(BF16)

    def finish(image, back):
        lanes = slice(image * width, (image + 1) * width)
        grad_input[:LATE, lanes] = back.astype(BF16)
        grad_input[LATE:, lanes] = edge[image].astype(BF16)

    stream_grad(images, False, stacked, wide, stream, grad_mid, gain_one, finish)


SMEM = pl.BlockSpec(memory_space=pltpu.SMEM)
VMEM = pl.BlockSpec(memory_space=pltpu.VMEM)
ANY = pl.BlockSpec(memory_space=pl.ANY)
HBM = pl.BlockSpec(memory_space=pltpu.HBM)


def cost(flops, nbytes):
    return pl.CostEstimate(
        flops=int(flops * COST_SCALE), bytes_accessed=int(nbytes * COST_SCALE), transcendentals=0
    )


def call(kernel, outs, scratch, estimate, scalars, operands, grant, aliases=None, waits=()):
    ahead = len(scalars) + len(operands)
    skip = lambda *refs: kernel(*refs[:ahead], *refs[ahead + len(waits) :])
    return pl.pallas_call(
        skip,
        in_specs=[SMEM] * len(scalars) + [VMEM] * len(operands) + [ANY] * len(waits),
        out_specs=[VMEM] * len(outs),
        out_shape=[jax.ShapeDtypeStruct(shape, kind) for shape, kind in outs],
        scratch_shapes=[pltpu.VMEM(shape, kind) for shape, kind in scratch],
        compiler_params=pltpu.CompilerParams(vmem_limit_bytes=grant << 20),
        cost_estimate=estimate,
        input_output_aliases=aliases or {},
    )(*scalars, *operands, *waits)


def saved_shapes(images, rows):
    return [
        ((3, 2, images, KEYS, 384), BF16),
        ((3, 2, images, ROWS, 2 * KEYS), BF16),
        ((3, rows, 256), BF16),
        ((3, rows, 256), F32),
    ]


def pack_weights(chunks, place, w_qkv, w_out, w_fc1, w_fc2):
    rows = w_fc1.shape[0]
    shapes = (rows, 768), (rows, 768 + 2 * chunks[1]), (rows, 2 * (chunks[0] + chunks[2]))
    return pl.pallas_call(
        functools.partial(pack_kernel, chunks),
        in_specs=[SMEM] + [HBM] * 4,
        out_specs=[VMEM] * 3,
        out_shape=[jax.ShapeDtypeStruct(shape, BF16) for shape in shapes],
        scratch_shapes=[
            pltpu.VMEM(w_qkv.shape, BF16),
            pltpu.VMEM(w_out.shape, BF16),
            pltpu.SemaphoreType.DMA((2 + 2 * len(chunks),)),
        ],
        compiler_params=pltpu.CompilerParams(vmem_limit_bytes=63 << 20),
        cost_estimate=cost(1e7, 1e7),
    )(place, w_qkv, w_out, w_fc1, w_fc2.T)


def prepare_tokens(place, lengths, tokens, prompts, key_mask, grads, gain, shift):
    images, _, width = tokens.shape
    rows = images * ROWS
    return call(
        functools.partial(token_kernel, images),
        [((rows, width), BF16)] * 3 + [((images, 1, KEYS), F32)],
        [((ROWS, width), F32)],
        cost(1e7, 1e7),
        (place, lengths),
        (tokens, prompts, key_mask, grads, gain, shift),
        4,
    )


def attend(loader, images, place, normed, visible, stream, b_out, gain, shift, pieces, waits):
    rows, width = normed.shape
    return call(
        functools.partial(attend_kernel, loader, images),
        saved_shapes(images, rows)
        + [((rows, width), F32), ((rows, width), BF16)]
        + [((3, width, 768), BF16), ((width, 768), BF16)],
        [((width, 1024), BF16)],
        cost(8e9, 1e7),
        (place,),
        (normed, visible, stream, b_out, gain, shift, *pieces),
        GRANTS[0],
        waits=waits,
    )


def mlp(loader, slots, place, normed, grad, bias, sums, pieces, waits):
    rows, width = normed.shape
    hidden = bias.shape[1]
    first = sums is None
    sums = () if first else tuple(sums)
    return call(
        functools.partial(mlp_kernel, loader, hidden // slots, slots, first),
        [((rows, width), F32)] * 2,
        [((width, hidden), BF16)] * 2,
        cost(8.0 * rows * width * hidden, 1.6e7),
        (place,),
        (normed, grad, bias, *sums, *pieces),
        GRANTS[2],
        {} if first else {4: 0, 5: 1},
        waits,
    )


def attend_back(
    images, give_kind, place, mid, grad_normed, grad, stream, saved, gain_two, gain_one, weights
):
    rows, width = mid.shape
    return call(
        functools.partial(back_kernel, images),
        [
            ((PROMPTS, width // 2), F32),
            ((PROMPTS, width // 2), give_kind),
            ((images, IMG_TOK - LATE, width), F32),
            ((rows, width), F32),
            ((rows, 3 * 768), BF16),
        ],
        [((rows, width), BF16), ((3, rows, 256), F32)],
        cost(9e9, 2.4e7),
        (place,),
        (mid, grad_normed, grad, stream, *saved, gain_two, gain_one, *weights),
        GRANTS[3],
    )


def finish_rows(images, place, lengths, mid, mlp_out, stream, b_fc2, gain_one, weights, passed):
    width = mid.shape[1]
    return call(
        functools.partial(last_kernel, images),
        [((SEQ, images * width), BF16), ((IMG_TOK, images * width), BF16)],
        [],
        cost(2e9, 1e7),
        (place, lengths),
        (mid, mlp_out, stream, b_fc2, gain_one, weights[0], *passed),
        7,
    )


def add_kernel(*refs):
    *parts, out = refs
    parts = [part[...].astype(F32) for part in parts]
    while len(parts) > 1:
        parts = [parts[at] + parts[at + 1] for at in range(0, len(parts), 2)]
    out[...] = parts[0].astype(BF16)


def add(*parts, waits=()):
    outs = [(parts[-1].shape, BF16)]
    return call(add_kernel, outs, [], cost(0, 0), (), parts, 1, waits=waits)[0]


def sum_prompts(exchange, keep, give, results):
    mine = add(keep, exchange.core(give))
    others = [exchange.swap(mine, dx=dx, dy=dy) for dx, dy in ((1, 0), (0, 1), (1, 1))]
    mine = add(mine, *others, waits=results)
    for dz in (1, 2):
        mine = add(mine, exchange.swap(mine, dz=dz))
    other = exchange.core(mine).astype(F32)
    mine = lax.reduce_precision(mine.astype(F32), 8, 7)
    return jnp.where(
        lax.axis_index("head") % 2 == 0,
        jnp.concatenate([mine, other], axis=1),
        jnp.concatenate([other, mine], axis=1),
    )


def per_device(
    exchange,
    layer_input,
    prompts,
    lengths,
    key_mask,
    ln1_gain,
    ln1_shift,
    w_qkv,
    w_out,
    b_out,
    ln2_gain,
    ln2_shift,
    w_fc1,
    b_fc1,
    w_fc2,
    b_fc2,
    grad_output,
):
    images, _, width = layer_input.shape
    chunks = CHUNKS
    head = lax.axis_index("head")
    core = head % 2

    if exchange is not None:
        depth = exchange.depth
        dp = lax.axis_index("dp")
        place = [dp // 2, dp % 2, head // 2, core]
    else:
        depth = 0
        place = [0, 0, 0, core]
    place = jnp.stack([jnp.asarray(value, jnp.int32) for value in (*place, head * images)])

    own, both, later = pack_weights(chunks, place, w_qkv, w_out, w_fc1, w_fc2)
    if exchange is not None:
        gather = Gather(exchange, own, both, later, b_fc1)
    else:

        def gather_whole(piece):
            rows = lax.all_gather(piece, "dp", axis=0, tiled=True)
            held = Held(None)
            held.arrays = [lax.all_gather(rows, "head", axis=0)]
            held.plan = [(0, ALL, [(dy, c) for dy in (0, 1) for c in (0, 1)])]
            return held

        attn = gather_whole(own)
        split = 2 * chunks[0]
        gathered = [gather_whole(piece) for piece in (later[:, :split], both[:, 768:], later[:, split:])]
        bias = lax.all_gather(b_fc1, "head", axis=0)

    row = lambda vector: vector.reshape(1, -1)
    stream, normed, grad, visible = prepare_tokens(
        place, lengths, layer_input, prompts, key_mask, grad_output, row(ln1_gain), row(ln1_shift)
    )
    waits = ()
    if exchange is not None:
        attn, (normed, visible, stream, grad) = gather.attention(normed, visible, stream, grad)
        bias = gather.bias
        waits = (bias,)
    load_attn = Loader(attn.plan, depth)
    *saved, mid, normed_mlp, wide, out = attend(
        load_attn, images, place, normed, visible, stream,
        row(b_out), row(ln2_gain), row(ln2_shift), attn.arrays, waits,
    )
    if exchange is None:
        order = [(bias, gathered[index], 4, index) for index in range(3)]
    else:
        normed_mlp = gather.round_seven(normed_mlp)
        even, odd = bias[0::2], bias[1::2]
        biases = jnp.where(core == 0, even, odd), jnp.where(core == 0, odd, even)
        both = Held(None)
        both.arrays = gather.halves[0].arrays + gather.halves[1].arrays
        both.plan = gather.halves[0].plan + gather.halves[1].plan
        order = [(bias, both, 4, 0)]
        order += [(bias, gather.parts[index], 4, index) for index in (1, 2)]
    sums = None
    for values, held, slots, index in order:
        if exchange is not None and index == 1:
            sums[0] = gather.round_eight(sums[0])
        chunk_bias = row(values[:, sum(chunks[:index]) : sum(chunks[: index + 1])])
        loader = Loader(held.plan, depth)
        sums = mlp(loader, slots, place, normed_mlp, grad, chunk_bias, sums, held.arrays, ())
        sums = list(sums)
    weights = (wide, out)
    keep, give, *passed = attend_back(
        images, BF16 if exchange is not None else F32, place, mid, sums[1], grad, stream, saved,
        row(ln2_gain), row(ln1_gain), weights,
    )
    results = finish_rows(
        images, place, lengths, mid, sums[0], stream, row(b_fc2), row(ln1_gain), weights, passed
    )
    if exchange is not None:
        total = sum_prompts(exchange, keep, give, results)
    else:
        total = lax.psum(jnp.concatenate([keep, give], axis=1), BOTH)
    results = [result.reshape(result.shape[0], images, width) for result in results]
    return (*(jnp.transpose(result, (1, 0, 2)) for result in results), total)


def solution(mesh):
    dp, head = mesh.shape["dp"], mesh.shape["head"]
    exchange = Exchange(dp, head) if (dp, head) == (8, 4) else None
    placed = (
        P(BOTH, None, None),
        P(),
        P("dp"),
        P("dp", None),
        P(),
        P(),
        P(None, "dp", "head"),
        P("head", "dp"),
        P(),
        P(),
        P(),
        P("dp", "head"),
        P("head"),
        P("head", "dp"),
        P(),
        P(BOTH, None, None),
    )
    return jax.shard_map(
        functools.partial(per_device, exchange),
        mesh=mesh,
        in_specs=placed,
        out_specs=(P(BOTH, None, None), P(BOTH, None, None), P()),
        check_vma=False,
    )
```

profile of v0, /device:TPU:0, one launch (start us, length us, event | category | flops | bytes accessed | tf_op | source)
XLA Modules:
  0.0 134.6 jit_solution(9377923308557159611)
XLA Ops:
  1.3 2.6 %shard_map.175 = (bf16[96,768]{1,0:T(8,128)(2,1)}, bf16[96,1280]{1,0:T(8,128)(2,1)}, bf16[96,1024]{1,0:T(8,128)(2,1)}) custom-call(s32[5]{0:T(128)} %stack.37.place.refs_0_, bf16[3,96,192]{2,1,0:T(8,128)(2,1)} %w_qkv.1, bf16[192,96]{1,0:T(8,128)(2,1)} %w_out.1, bf16[96,768]{1,0:T(8,128)(2,1)} %w_fc1.1, bf16[96,768]{1,0:T(8,128)(2,1)} %bitcast.33), custom_call_target="tpu_custom_call" | custom-call | flops 100000000 | bytes 100000000 | tf_op jit(solution)/shard_map/pallas_call | solution.py:567
  3.9 3.1 %collective-permute-start.2 = (bf16[1,96,768]{2,1,0:T(8,128)(2,1)}, bf16[1,96,768]{2,1,0:T(8,128)(2,1)S(1)}, u32[]{:S(2)}, u32[]{:S(2)}) collective-permute-start(bf16[1,96,768]{2,1,0:T(8,128)(2,1)} %bitcast.34), channel_id=1, source_target_pairs={{0,8},{1,9},{2,10},{3,11},{4,12},{5,13},{6,14},{7,15},{8,24},{9,25... | collective-permute-start | bytes 442376 | tf_op jit(solution)/shard_map/ppermute | solution.py:53
  7.0 1.1 collective-permute-start.1
  8.1 1.8 %collective-permute-start = (bf16[1,96,1280]{2,1,0:T(8,128)(2,1)}, bf16[1,96,1280]{2,1,0:T(8,128)(2,1)S(1)}, u32[]{:S(2)}, u32[]{:S(2)}) collective-permute-start(bf16[1,96,1280]{2,1,0:T(8,128)(2,1)} %bitcast.28), channel_id=1, source_target_pairs={{0,4},{1,3},{2,6},{3,1},{4,0},{5,7},{6,2},{7,5},{8,12},{9,11},{10,... | collective-permute-start | bytes 737288 | tf_op jit(solution)/shard_map/ppermute | solution.py:53
  9.9 2.3 %collective-permute-done.2 = bf16[1,96,768]{2,1,0:T(8,128)(2,1)S(1)} collective-permute-done((bf16[1,96,768]{2,1,0:T(8,128)(2,1)}, bf16[1,96,768]{2,1,0:T(8,128)(2,1)S(1)}, u32[]{:S(2)}, u32[]{:S(2)}) %collective-permute-start.2) | collective-permute-done | bytes 147488 | tf_op jit(solution)/shard_map/ppermute | solution.py:53
  12.2 3.1 %collective-permute-done.1 = bf16[1,96,768]{2,1,0:T(8,128)(2,1)S(1)} collective-permute-done((bf16[1,96,768]{2,1,0:T(8,128)(2,1)}, bf16[1,96,768]{2,1,0:T(8,128)(2,1)S(1)}, u32[]{:S(2)}, u32[]{:S(2)}) %collective-permute-start.1) | collective-permute-done | bytes 147488 | tf_op jit(solution)/shard_map/ppermute | solution.py:53
  15.3 1.0 constant_dynamic-update-slice_fusion.1
  16.4 1.6 %collective-permute-start.3 = (bf16[2,96,1280]{2,1,0:T(8,128)(2,1)S(1)}, bf16[2,96,1280]{2,1,0:T(8,128)(2,1)S(1)}, u32[]{:S(2)}, u32[]{:S(2)}) collective-permute-start(bf16[2,96,1280]{2,1,0:T(8,128)(2,1)S(1)} %constant_dynamic-update-slice_fusion.refs_7_.refs_6_), channel_id=1, source_target_pairs={{0,2},{1,5},{2,0},{3,7},{4,6},{5,1},{6,4},{7,3},{8,10},{9,13},{10,... | collective-permute-start | bytes 1474568 | tf_op jit(solution)/shard_map/ppermute | solution.py:53
  18.0 0.7 slice.30
  18.7 1.7 %collective-permute-start.4 = (bf16[1,96,768]{2,1,0:T(8,128)(2,1)}, bf16[1,96,768]{2,1,0:T(8,128)(2,1)S(1)}, u32[]{:S(2)}, u32[]{:S(2)}) collective-permute-start(bf16[1,96,768]{2,1,0:T(8,128)(2,1)} %slice.30), channel_id=1, source_target_pairs={{0,16},{1,17},{2,18},{3,19},{4,20},{5,21},{6,22},{7,23},{8,0},{9,1... | collective-permute-start | bytes 442376 | tf_op jit(solution)/shard_map/ppermute | solution.py:53
  21.2 1.6 %shard_map.176 = (bf16[608,768]{1,0:T(8,128)(2,1)S(1)}, bf16[608,768]{1,0:T(8,128)(2,1)S(1)}, bf16[608,768]{1,0:T(8,128)(2,1)S(1)}, f32[2,1,384]{2,1,0:T(1,128)S(1)}) custom-call(s32[5]{0:T(128)S(1)} %copy-done.4, s32[8]{0:T(128)S(1)} %copy-done.5, bf16[2,197,768]{2,1,0:T(8,128)(2,1)S(1)} %copy.23.refs_2_, bf16[100,768]{1,0:T(8,128)(2,1)S(1)} %copy-done, ...), custom_call_target="tpu_custom_call" | custom-call | flops 100000000 | bytes 100000000 | tf_op jit(solution)/shard_map/pallas_call | solution.py:543
  22.8 1.0 copy-done.7
  24.4 0.9 collective-permute-done.3.refs_8_.refs_7_
  25.3 1.5 %collective-permute-start.6 = (bf16[3,96,768]{2,1,0:T(8,128)(2,1)S(1)}, bf16[3,96,768]{2,1,0:T(8,128)(2,1)S(1)}, u32[]{:S(2)}, u32[]{:S(2)}) collective-permute-start(bf16[3,96,768]{2,1,0:T(8,128)(2,1)S(1)} %pad_maximum_fusion.3), channel_id=1, source_target_pairs={{0,4},{1,3},{2,6},{3,1},{4,0},{5,7},{6,2},{7,5},{8,12},{9,11},{10,... | collective-permute-start | bytes 1327112 | tf_op jit(solution)/shard_map/ppermute | solution.py:53
  27.3 1.7 %collective-permute-start.7 = (bf16[1,96,1024]{2,1,0:T(8,128)(2,1)S(1)}, bf16[1,96,1024]{2,1,0:T(8,128)(2,1)S(1)}, u32[]{:S(2)}, u32[]{:S(2)}) collective-permute-start(bf16[1,96,1024]{2,1,0:T(8,128)(2,1)S(1)} %bitcast.30), channel_id=1, source_target_pairs={{0,16},{1,17},{2,18},{3,19},{4,20},{5,21},{6,22},{7,23},{8,0},{9,1... | collective-permute-start | bytes 589832 | tf_op jit(solution)/shard_map/ppermute | solution.py:53
  29.0 4.6 %collective-permute-done.6 = bf16[3,96,768]{2,1,0:T(8,128)(2,1)S(1)} collective-permute-done((bf16[3,96,768]{2,1,0:T(8,128)(2,1)S(1)}, bf16[3,96,768]{2,1,0:T(8,128)(2,1)S(1)}, u32[]{:S(2)}, u32[]{:S(2)}) %collective-permute-start.6) | collective-permute-done | bytes 442400 | tf_op jit(solution)/shard_map/ppermute | solution.py:53
  34.1 1.5 %collective-permute-start.11 = (bf16[6,96,768]{2,1,0:T(8,128)(2,1)S(1)}, bf16[6,96,768]{2,1,0:T(8,128)(2,1)S(1)}, u32[]{:S(2)}, u32[]{:S(2)}) collective-permute-start(bf16[6,96,768]{2,1,0:T(8,128)(2,1)S(1)} %pad_maximum_fusion.1.refs_11_), channel_id=1, source_target_pairs={{0,2},{1,5},{2,0},{3,7},{4,6},{5,1},{6,4},{7,3},{8,10},{9,13},{10,... | collective-permute-start | bytes 2654216 | tf_op jit(solution)/shard_map/ppermute | solution.py:53
  35.7 2.6 %collective-permute-start.13 = (bf16[1,96,1024]{2,1,0:T(8,128)(2,1)S(1)}, bf16[1,96,1024]{2,1,0:T(8,128)(2,1)S(1)}, u32[]{:S(2)}, u32[]{:S(2)}) collective-permute-start(bf16[1,96,1024]{2,1,0:T(8,128)(2,1)S(1)} %collective-permute-done.7), channel_id=1, source_target_pairs={{0,16},{1,17},{2,18},{3,19},{4,20},{5,21},{6,22},{7,23},{8,0},{9,1... | collective-permute-start | bytes 589832 | tf_op jit(solution)/shard_map/ppermute | solution.py:53
  38.9 8.4 %collective-permute-done.14 = f32[2,768]{1,0:T(2,128)S(1)} collective-permute-done((f32[2,768]{1,0:T(2,128)S(1)}, f32[2,768]{1,0:T(2,128)S(1)}, u32[]{:S(2)}, u32[]{:S(2)}) %collective-permute-start.14) | collective-permute-done | bytes 6176 | tf_op jit(solution)/shard_map/ppermute | solution.py:53
  47.7 1.5 %collective-permute-start.16 = (bf16[4,96,1024]{2,1,0:T(8,128)(2,1)S(1)}, bf16[4,96,1024]{2,1,0:T(8,128)(2,1)S(1)}, u32[]{:S(2)}, u32[]{:S(2)}) collective-permute-start(bf16[4,96,1024]{2,1,0:T(8,128)(2,1)S(1)} %pad_maximum_fusion.2), channel_id=1, source_target_pairs={{0,4},{1,3},{2,6},{3,1},{4,0},{5,7},{6,2},{7,5},{8,12},{9,11},{10,... | collective-permute-start | bytes 2359304 | tf_op jit(solution)/shard_map/ppermute | solution.py:53
  49.7 1.5 %collective-permute-start.17 = (bf16[4,96,512]{2,1,0:T(8,128)(2,1)S(1)}, bf16[4,96,512]{2,1,0:T(8,128)(2,1)S(1)}, u32[]{:S(2)}, u32[]{:S(2)}) collective-permute-start(bf16[4,96,512]{2,1,0:T(8,128)(2,1)S(1)} %pad_maximum_fusion.4), channel_id=1, source_target_pairs={{0,16},{1,17},{2,18},{3,19},{4,20},{5,21},{6,22},{7,23},{8,0},{9,1... | collective-permute-start | bytes 1179656 | tf_op jit(solution)/shard_map/ppermute | solution.py:53
  51.2 8.5 %collective-permute-done.16 = bf16[4,96,1024]{2,1,0:T(8,128)(2,1)S(1)} collective-permute-done((bf16[4,96,1024]{2,1,0:T(8,128)(2,1)S(1)}, bf16[4,96,1024]{2,1,0:T(8,128)(2,1)S(1)}, u32[]{:S(2)}, u32[]{:S(2)}) %collective-permute-start.16) | collective-permute-done | bytes 786464 | tf_op jit(solution)/shard_map/ppermute | solution.py:53
  59.9 0.8 collective-permute-done.17.refs_10_
  60.9 1.9 %collective-permute-start.18 = (bf16[8,96,768]{2,1,0:T(8,128)(2,1)S(1)}, bf16[8,96,768]{2,1,0:T(8,128)(2,1)S(1)}, u32[]{:S(2)}, u32[]{:S(2)}) collective-permute-start(bf16[8,96,768]{2,1,0:T(8,128)(2,1)S(1)} %slice.33), channel_id=1, source_target_pairs={{0,2},{1,5},{2,0},{3,7},{4,6},{5,1},{6,4},{7,3},{8,10},{9,13},{10,... | collective-permute-start | bytes 3538952 | tf_op jit(solution)/shard_map/ppermute | solution.py:53
  62.8 2.3 %collective-permute-start.19 = (bf16[4,96,512]{2,1,0:T(8,128)(2,1)S(1)}, bf16[4,96,512]{2,1,0:T(8,128)(2,1)S(1)}, u32[]{:S(2)}, u32[]{:S(2)}) collective-permute-start(bf16[4,96,512]{2,1,0:T(8,128)(2,1)S(1)} %pad_maximum_fusion.4), channel_id=1, source_target_pairs={{0,8},{1,9},{2,10},{3,11},{4,12},{5,13},{6,14},{7,15},{8,24},{9,25... | collective-permute-start | bytes 1179656 | tf_op jit(solution)/shard_map/ppermute | solution.py:53
  65.1 0.7 collective-permute-start.20
  65.8 10.1 %shard_map.177 = (bf16[3,2,2,384,384]{4,3,2,1,0:T(8,128)(2,1)S(1)}, bf16[3,2,2,304,768]{4,3,2,1,0:T(8,128)(2,1)S(1)}, bf16[3,608,256]{2,1,0:T(8,128)(2,1)S(1)}, ...) custom-call(s32[5]{0:T(128)S(1)} %copy-done.4, ...), custom_call_target="tpu_custom_call" | custom-call | flops 80000000000 | bytes 100000000 | tf_op jit(solution)/shard_map/pallas_call | solution.py:543
  75.8 2.8 %collective-permute-done.20.refs_14_ = bf16[2,96,512]{2,1,0:T(8,128)(2,1)S(1)} collective-permute-done((bf16[2,96,512]{2,1,0:T(8,128)(2,1)S(1)}, bf16[2,96,512]{2,1,0:T(8,128)(2,1)S(1)}, u32[]{:S(2)}, u32[]{:S(2)}) %collective-permute-start.20) | collective-permute-done | bytes 196640 | tf_op jit(solution)/shard_map/ppermute | solution.py:53
  79.3 1.6 %collective-permute-start.21 = (bf16[2,96,512]{2,1,0:T(8,128)(2,1)S(1)}, bf16[2,96,512]{2,1,0:T(8,128)(2,1)S(1)}, u32[]{:S(2)}, u32[]{:S(2)}) collective-permute-start(bf16[2,96,512]{2,1,0:T(8,128)(2,1)S(1)} %slice.37), channel_id=1, source_target_pairs={{0,8},{1,9},{2,10},{3,11},{4,12},{5,13},{6,14},{7,15},{8,24},{9,25... | collective-permute-start | bytes 589832 | tf_op jit(solution)/shard_map/ppermute | solution.py:53
  80.9 1.2 collective-permute-start.22
  82.7 5.1 %shard_map.178 = (f32[608,768]{1,0:T(8,128)S(1)}, f32[608,768]{1,0:T(8,128)S(1)}) custom-call(s32[5]{0:T(128)S(1)} %copy-done.4, bf16[608,768]{1,0:T(8,128)(2,1)S(1)} %get-tuple-element.106.refs_1_, bf16[608,768]{1,0:T(8,128)(2,1)S(1)} %get-tuple-element.107.refs_2_.refs_3_, f32[1,1024]{1,0:T(1,128)S(1)} %bitcast.25, ...), custom_call_target="tpu_custom_call" | custom-call | flops 38252052480 | bytes 160000000 | tf_op jit(solution)/shard_map/pallas_call | solution.py:543
  87.8 0.9 collective-permute-done.22.refs_10_
  89.3 0.8 collective-permute-done.28.refs_17_
  90.2 5.0 %shard_map.179 = (f32[608,768]{1,0:T(8,128)S(1)}, f32[608,768]{1,0:T(8,128)S(1)}) custom-call(s32[5]{0:T(128)S(1)} %copy-done.4, bf16[608,768]{1,0:T(8,128)(2,1)S(1)} %get-tuple-element.106.refs_1_, bf16[608,768]{1,0:T(8,128)(2,1)S(1)} %get-tuple-element.107.refs_2_.refs_3_, f32[1,1024]{1,0:T(1,128)S(1)} %bitcast.24, ...), custom_call_target="tpu_custom_call", output_to_operand_aliasing={{0}: (4, {}), {1}: (5, {})} | custom-call | flops 38252052480 | bytes 160000000 | tf_op jit(solution)/shard_map/pallas_call | solution.py:543
  95.3 5.2 %shard_map.180 = (f32[608,768]{1,0:T(8,128)S(1)}, f32[608,768]{1,0:T(8,128)S(1)}) custom-call(s32[5]{0:T(128)S(1)} %copy-done.4, bf16[608,768]{1,0:T(8,128)(2,1)S(1)} %get-tuple-element.106.refs_1_, bf16[608,768]{1,0:T(8,128)(2,1)S(1)} %get-tuple-element.107.refs_2_.refs_3_, f32[1,1024]{1,0:T(1,128)S(1)} %bitcast.23, ...), custom_call_target="tpu_custom_call", output_to_operand_aliasing={{0}: (4, {}), {1}: (5, {})} | custom-call | flops 38252052480 | bytes 160000000 | tf_op jit(solution)/shard_map/pallas_call | solution.py:543
  100.5 12.7 %shard_map.181 = (f32[100,384]{1,0:T(8,128)S(1)}, bf16[100,384]{1,0:T(8,128)(2,1)S(1)}, f32[2,5,768]{2,1,0:T(8,128)S(1)}, f32[608,768]{1,0:T(8,128)S(1)}, bf16[608,2304]{1,0:T(8,128)(2,1)S(1)}) custom-call(s32[5]{0:T(128)S(1)} %copy-done.4, f32[608,768]{1,0:T(8,128)S(1)} %get-tuple-element.99.refs_1_.refs_2_, f32[608,768]{1,0:T(8,128)S(1)} %get-tuple-element.122.refs_2_, ...), custom_call_target="tpu_custom_call" | custom-call | flops 89999998976 | bytes 240000000 | tf_op jit(solution)/shard_map/pallas_call | solution.py:543
  113.4 1.1 collective-permute-done.30.refs_1_
  114.6 0.9 collective-permute-start.31
  115.5 1.7 %collective-permute-start.32 = (bf16[100,384]{1,0:T(8,128)(2,1)S(1)}, bf16[100,384]{1,0:T(8,128)(2,1)S(1)}, u32[]{:S(2)}, u32[]{:S(2)}) collective-permute-start(bf16[100,384]{1,0:T(8,128)(2,1)S(1)} %shard_map.183.refs_0_), channel_id=1, source_target_pairs={{0,2},{1,3},{2,0},{3,1},{4,6},{5,7},{6,4},{7,5},{8,10},{9,11},{10,... | collective-permute-start | bytes 230408 | tf_op jit(solution)/shard_map/ppermute | solution.py:53
  117.1 1.0 collective-permute-start.33
  118.1 3.8 %shard_map.182 = (bf16[297,1536]{1,0:T(8,128)(2,1)S(1)}, bf16[197,1536]{1,0:T(8,128)(2,1)S(1)}) custom-call(s32[5]{0:T(128)S(1)} %copy-done.4, s32[8]{0:T(128)S(1)} %copy-done.6, f32[608,768]{1,0:T(8,128)S(1)} %get-tuple-element.99.refs_1_.refs_2_, f32[608,768]{1,0:T(8,128)S(1)} %get-tuple-element.120.refs_3_, ...), custom_call_target="tpu_custom_call" | custom-call | flops 20000000000 | bytes 100000000 | tf_op jit(solution)/shard_map/pallas_call | solution.py:543
  122.5 1.4 %collective-permute-start.34 = (bf16[100,384]{1,0:T(8,128)(2,1)S(1)}, bf16[100,384]{1,0:T(8,128)(2,1)S(1)}, u32[]{:S(2)}, u32[]{:S(2)}) collective-permute-start(bf16[100,384]{1,0:T(8,128)(2,1)S(1)} %shard_map.184.refs_0_), channel_id=1, source_target_pairs={{0,8},{1,9},{2,10},{3,11},{4,12},{5,13},{6,14},{7,15},{8,0},{9,1},... | collective-permute-start | bytes 230408 | tf_op jit(solution)/shard_map/ppermute | solution.py:53
  123.9 3.1 %collective-permute-done.34.refs_1_ = bf16[100,384]{1,0:T(8,128)(2,1)S(1)} collective-permute-done((bf16[100,384]{1,0:T(8,128)(2,1)S(1)}, bf16[100,384]{1,0:T(8,128)(2,1)S(1)}, u32[]{:S(2)}, u32[]{:S(2)}) %collective-permute-start.34) | collective-permute-done | bytes 76832 | tf_op jit(solution)/shard_map/ppermute | solution.py:53
  127.0 1.3 collective-permute-start.35
  128.3 2.2 %reshape.51 = bf16[297,2,768]{2,1,0:T(2,128)(2,1)} reshape(bf16[297,1536]{1,0:T(8,128)(2,1)S(1)} %get-tuple-element.131.refs_4_) | data formatting | bytes 1824768 | tf_op jit(solution)/shard_map/reshape | solution.py:787
  130.6 1.7 %reshape.52 = bf16[197,2,768]{2,1,0:T(2,128)(2,1)} reshape(bf16[197,1536]{1,0:T(8,128)(2,1)S(1)} %get-tuple-element.132.refs_5_) | data formatting | bytes 1210368 | tf_op jit(solution)/shard_map/reshape | solution.py:787
  132.5 1.2 collective-permute-done.36
  133.8 0.7 maximum_select_fusion
  (113 shorter events, 7.9 us)
Async XLA Ops:
  0.6 19.8 %copy-start.9 = (bf16[2,297,768]{2,0,1:T(2,128)(2,1)S(1)}, bf16[2,297,768]{2,0,1:T(2,128)(2,1)}, u32[]{:S(2)}) copy-start(bf16[2,297,768]{2,0,1:T(2,128)(2,1)} %param.31) | copy-start | bytes 2737156
  3.9 16.4 %copy-start.10 = (bf16[2,197,768]{2,0,1:T(2,128)(2,1)S(1)}, bf16[2,197,768]{2,0,1:T(2,128)(2,1)}, u32[]{:S(2)}) copy-start(bf16[2,197,768]{2,0,1:T(2,128)(2,1)} %param.16) | copy-start | bytes 1815556
  3.9 8.3 %collective-permute-start.2 = (bf16[1,96,768]{2,1,0:T(8,128)(2,1)}, bf16[1,96,768]{2,1,0:T(8,128)(2,1)S(1)}, u32[]{:S(2)}, u32[]{:S(2)}) collective-permute-start(bf16[1,96,768]{2,1,0:T(8,128)(2,1)} %bitcast.34), channel_id=1, source_target_pairs={{0,8},{1,9},{2,10},{3,11},{4,12},{5,13},{6,14},{7,15},{8,24},{9,25... | collective-permute-start | bytes 442376 | tf_op jit(solution)/shard_map/ppermute | solution.py:53
  7.0 8.2 %collective-permute-start.1 = (bf16[1,96,768]{2,1,0:T(8,128)(2,1)}, bf16[1,96,768]{2,1,0:T(8,128)(2,1)S(1)}, u32[]{:S(2)}, u32[]{:S(2)}) collective-permute-start(bf16[1,96,768]{2,1,0:T(8,128)(2,1)} %bitcast.35), channel_id=1, source_target_pairs={{0,16},{1,17},{2,18},{3,19},{4,20},{5,21},{6,22},{7,23},{8,0},{9,1... | collective-permute-start | bytes 442376 | tf_op jit(solution)/shard_map/ppermute | solution.py:53
  8.1 7.2 %collective-permute-start = (bf16[1,96,1280]{2,1,0:T(8,128)(2,1)}, bf16[1,96,1280]{2,1,0:T(8,128)(2,1)S(1)}, u32[]{:S(2)}, u32[]{:S(2)}) collective-permute-start(bf16[1,96,1280]{2,1,0:T(8,128)(2,1)} %bitcast.28), channel_id=1, source_target_pairs={{0,4},{1,3},{2,6},{3,1},{4,0},{5,7},{6,2},{7,5},{8,12},{9,11},{10,... | collective-permute-start | bytes 737288 | tf_op jit(solution)/shard_map/ppermute | solution.py:53
  16.3 4.9 %copy-start = (bf16[100,768]{1,0:T(8,128)(2,1)S(1)}, bf16[100,768]{1,0:T(8,128)(2,1)}, u32[]{:S(2)}) copy-start(bf16[100,768]{1,0:T(8,128)(2,1)} %refs_3_.1) | copy-start | bytes 460804
  16.4 8.9 %collective-permute-start.3 = (bf16[2,96,1280]{2,1,0:T(8,128)(2,1)S(1)}, bf16[2,96,1280]{2,1,0:T(8,128)(2,1)S(1)}, u32[]{:S(2)}, u32[]{:S(2)}) collective-permute-start(bf16[2,96,1280]{2,1,0:T(8,128)(2,1)S(1)} %constant_dynamic-update-slice_fusion.refs_7_.refs_6_), channel_id=1, source_target_pairs={{0,2},{1,5},{2,0},{3,7},{4,6},{5,1},{6,4},{7,3},{8,10},{9,13},{10,... | collective-permute-start | bytes 1474568 | tf_op jit(solution)/shard_map/ppermute | solution.py:53
  18.7 5.7 %collective-permute-start.4 = (bf16[1,96,768]{2,1,0:T(8,128)(2,1)}, bf16[1,96,768]{2,1,0:T(8,128)(2,1)S(1)}, u32[]{:S(2)}, u32[]{:S(2)}) collective-permute-start(bf16[1,96,768]{2,1,0:T(8,128)(2,1)} %slice.30), channel_id=1, source_target_pairs={{0,16},{1,17},{2,18},{3,19},{4,20},{5,21},{6,22},{7,23},{8,0},{9,1... | collective-permute-start | bytes 442376 | tf_op jit(solution)/shard_map/ppermute | solution.py:53
  20.4 6.9 %copy-start.11 = (bf16[96,1024]{1,0:T(8,128)(2,1)S(1)}, bf16[96,1024]{1,0:T(8,128)(2,1)}, u32[]{:S(2)}) copy-start(bf16[96,1024]{1,0:T(8,128)(2,1)} %get-tuple-element.71) | copy-start | bytes 589828
  20.6 3.1 %collective-permute-start.5 = (f32[768]{0:T(1024)S(1)}, f32[768]{0:T(1024)S(1)}, u32[]{:S(2)}, u32[]{:S(2)}) collective-permute-start(f32[768]{0:T(1024)S(1)} %copy-done.14), channel_id=1, source_target_pairs={{0,1},{1,0},{2,3},{3,2},{4,5},{5,4},{6,7},{7,6},{8,9},{9,8},{10,11... | collective-permute-start | bytes 9224 | tf_op jit(solution)/shard_map/ppermute | solution.py:53
  25.3 8.3 %collective-permute-start.6 = (bf16[3,96,768]{2,1,0:T(8,128)(2,1)S(1)}, bf16[3,96,768]{2,1,0:T(8,128)(2,1)S(1)}, u32[]{:S(2)}, u32[]{:S(2)}) collective-permute-start(bf16[3,96,768]{2,1,0:T(8,128)(2,1)S(1)} %pad_maximum_fusion.3), channel_id=1, source_target_pairs={{0,4},{1,3},{2,6},{3,1},{4,0},{5,7},{6,2},{7,5},{8,12},{9,11},{10,... | collective-permute-start | bytes 1327112 | tf_op jit(solution)/shard_map/ppermute | solution.py:53
  26.8 7.3 %collective-permute-start.8 = (bf16[2,96,1280]{2,1,0:T(8,128)(2,1)S(1)}, bf16[2,96,1280]{2,1,0:T(8,128)(2,1)S(1)}, u32[]{:S(2)}, u32[]{:S(2)}) collective-permute-start(bf16[2,96,1280]{2,1,0:T(8,128)(2,1)S(1)} %constant_dynamic-update-slice_fusion.refs_7_.refs_6_), channel_id=1, source_target_pairs={{0,1},{1,0},{2,3},{3,2},{4,5},{5,4},{6,7},{7,6},{8,9},{9,8},{10,11... | collective-permute-start | bytes 1474568 | tf_op jit(solution)/shard_map/ppermute | solution.py:53
  26.8 7.3 %collective-permute-start.9 = (bf16[2,96,1280]{2,1,0:T(8,128)(2,1)S(1)}, bf16[2,96,1280]{2,1,0:T(8,128)(2,1)S(1)}, u32[]{:S(2)}, u32[]{:S(2)}) collective-permute-start(bf16[2,96,1280]{2,1,0:T(8,128)(2,1)S(1)} %collective-permute-done.3.refs_8_.refs_7_), channel_id=1, source_target_pairs={{0,1},{1,0},{2,3},{3,2},{4,5},{5,4},{6,7},{7,6},{8,9},{9,8},{10,11... | collective-permute-start | bytes 1474568 | tf_op jit(solution)/shard_map/ppermute | solution.py:53
  27.3 6.8 %collective-permute-start.7 = (bf16[1,96,1024]{2,1,0:T(8,128)(2,1)S(1)}, bf16[1,96,1024]{2,1,0:T(8,128)(2,1)S(1)}, u32[]{:S(2)}, u32[]{:S(2)}) collective-permute-start(bf16[1,96,1024]{2,1,0:T(8,128)(2,1)S(1)} %bitcast.30), channel_id=1, source_target_pairs={{0,16},{1,17},{2,18},{3,19},{4,20},{5,21},{6,22},{7,23},{8,0},{9,1... | collective-permute-start | bytes 589832 | tf_op jit(solution)/shard_map/ppermute | solution.py:53
  33.7 17.5 %copy-start.15 = (f32[768]{0:T(1024)S(1)}, f32[768]{0:T(1024)}, u32[]{:S(2)}) copy-start(f32[768]{0:T(1024)} %param.24) | copy-start | bytes 9220
  33.7 17.5 %copy-start.16 = (f32[768]{0:T(1024)S(1)}, f32[768]{0:T(1024)}, u32[]{:S(2)}) copy-start(f32[768]{0:T(1024)} %param.25) | copy-start | bytes 9220
  33.7 17.5 %copy-start.17 = (f32[768]{0:T(1024)S(1)}, f32[768]{0:T(1024)}, u32[]{:S(2)}) copy-start(f32[768]{0:T(1024)} %param.26) | copy-start | bytes 9220
  34.1 13.5 %collective-permute-start.11 = (bf16[6,96,768]{2,1,0:T(8,128)(2,1)S(1)}, bf16[6,96,768]{2,1,0:T(8,128)(2,1)S(1)}, u32[]{:S(2)}, u32[]{:S(2)}) collective-permute-start(bf16[6,96,768]{2,1,0:T(8,128)(2,1)S(1)} %pad_maximum_fusion.1.refs_11_), channel_id=1, source_target_pairs={{0,2},{1,5},{2,0},{3,7},{4,6},{5,1},{6,4},{7,3},{8,10},{9,13},{10,... | collective-permute-start | bytes 2654216 | tf_op jit(solution)/shard_map/ppermute | solution.py:53
  35.7 11.7 %collective-permute-start.13 = (bf16[1,96,1024]{2,1,0:T(8,128)(2,1)S(1)}, bf16[1,96,1024]{2,1,0:T(8,128)(2,1)S(1)}, u32[]{:S(2)}, u32[]{:S(2)}) collective-permute-start(bf16[1,96,1024]{2,1,0:T(8,128)(2,1)S(1)} %collective-permute-done.7), channel_id=1, source_target_pairs={{0,16},{1,17},{2,18},{3,19},{4,20},{5,21},{6,22},{7,23},{8,0},{9,1... | collective-permute-start | bytes 589832 | tf_op jit(solution)/shard_map/ppermute | solution.py:53
  38.2 9.3 %collective-permute-start.12 = (bf16[1,96,1024]{2,1,0:T(8,128)(2,1)S(1)}, bf16[1,96,1024]{2,1,0:T(8,128)(2,1)S(1)}, u32[]{:S(2)}, u32[]{:S(2)}) collective-permute-start(bf16[1,96,1024]{2,1,0:T(8,128)(2,1)S(1)} %bitcast.31), channel_id=1, source_target_pairs={{0,8},{1,9},{2,10},{3,11},{4,12},{5,13},{6,14},{7,15},{8,24},{9,25... | collective-permute-start | bytes 589832 | tf_op jit(solution)/shard_map/ppermute | solution.py:53
  38.5 8.8 %collective-permute-start.14 = (f32[2,768]{1,0:T(2,128)S(1)}, f32[2,768]{1,0:T(2,128)S(1)}, u32[]{:S(2)}, u32[]{:S(2)}) collective-permute-start(f32[2,768]{1,0:T(2,128)S(1)} %maximum_select_fusion.1), channel_id=1, source_target_pairs={{0,2},{1,3},{2,0},{3,1},{4,6},{5,7},{6,4},{7,5},{8,10},{9,11},{10,... | collective-permute-start | bytes 18440 | tf_op jit(solution)/shard_map/ppermute | solution.py:53
  47.7 12.1 %collective-permute-start.16 = (bf16[4,96,1024]{2,1,0:T(8,128)(2,1)S(1)}, bf16[4,96,1024]{2,1,0:T(8,128)(2,1)S(1)}, u32[]{:S(2)}, u32[]{:S(2)}) collective-permute-start(bf16[4,96,1024]{2,1,0:T(8,128)(2,1)S(1)} %pad_maximum_fusion.2), channel_id=1, source_target_pairs={{0,4},{1,3},{2,6},{3,1},{4,0},{5,7},{6,2},{7,5},{8,12},{9,11},{10,... | collective-permute-start | bytes 2359304 | tf_op jit(solution)/shard_map/ppermute | solution.py:53
  49.2 15.9 %collective-permute-start.10 = (bf16[6,96,768]{2,1,0:T(8,128)(2,1)S(1)}, bf16[6,96,768]{2,1,0:T(8,128)(2,1)S(1)}, u32[]{:S(2)}, u32[]{:S(2)}) collective-permute-start(bf16[6,96,768]{2,1,0:T(8,128)(2,1)S(1)} %pad_maximum_fusion.1.refs_11_), channel_id=1, source_target_pairs={{0,1},{1,0},{2,3},{3,2},{4,5},{5,4},{6,7},{7,6},{8,9},{9,8},{10,11... | collective-permute-start | bytes 2654216 | tf_op jit(solution)/shard_map/ppermute | solution.py:53
  49.2 16.6 %collective-permute-start.15 = (bf16[6,96,768]{2,1,0:T(8,128)(2,1)S(1)}, bf16[6,96,768]{2,1,0:T(8,128)(2,1)S(1)}, u32[]{:S(2)}, u32[]{:S(2)}) collective-permute-start(bf16[6,96,768]{2,1,0:T(8,128)(2,1)S(1)} %collective-permute-done.11.refs_13_), channel_id=1, source_target_pairs={{0,1},{1,0},{2,3},{3,2},{4,5},{5,4},{6,7},{7,6},{8,9},{9,8},{10,11... | collective-permute-start | bytes 2654216 | tf_op jit(solution)/shard_map/ppermute | solution.py:53
  49.7 11.0 %collective-permute-start.17 = (bf16[4,96,512]{2,1,0:T(8,128)(2,1)S(1)}, bf16[4,96,512]{2,1,0:T(8,128)(2,1)S(1)}, u32[]{:S(2)}, u32[]{:S(2)}) collective-permute-start(bf16[4,96,512]{2,1,0:T(8,128)(2,1)S(1)} %pad_maximum_fusion.4), channel_id=1, source_target_pairs={{0,16},{1,17},{2,18},{3,19},{4,20},{5,21},{6,22},{7,23},{8,0},{9,1... | collective-permute-start | bytes 1179656 | tf_op jit(solution)/shard_map/ppermute | solution.py:53
  59.9 5.9 %copy-start.8 = (bf16[608,768]{1,0:T(8,128)(2,1)S(1)}, bf16[608,768]{1,0:T(8,128)(2,1)}, u32[]{:S(2)}) copy-start(bf16[608,768]{1,0:T(8,128)(2,1)} %copy-done.7) | copy-start | bytes 2801668
  60.8 21.3 %collective-permute-start.23 = (bf16[8,96,1024]{2,1,0:T(8,128)(2,1)S(1)}, bf16[8,96,1024]{2,1,0:T(8,128)(2,1)S(1)}, u32[]{:S(2)}, u32[]{:S(2)}) collective-permute-start(bf16[8,96,1024]{2,1,0:T(8,128)(2,1)S(1)} %pad_maximum_fusion.refs_4_.refs_6_), channel_id=1, source_target_pairs={{0,1},{1,0},{2,3},{3,2},{4,5},{5,4},{6,7},{7,6},{8,9},{9,8},{10,11... | collective-permute-start | bytes 4718600 | tf_op jit(solution)/shard_map/ppermute | solution.py:53
  60.9 17.7 %collective-permute-start.18 = (bf16[8,96,768]{2,1,0:T(8,128)(2,1)S(1)}, bf16[8,96,768]{2,1,0:T(8,128)(2,1)S(1)}, u32[]{:S(2)}, u32[]{:S(2)}) collective-permute-start(bf16[8,96,768]{2,1,0:T(8,128)(2,1)S(1)} %slice.33), channel_id=1, source_target_pairs={{0,2},{1,5},{2,0},{3,7},{4,6},{5,1},{6,4},{7,3},{8,10},{9,13},{10,... | collective-permute-start | bytes 3538952 | tf_op jit(solution)/shard_map/ppermute | solution.py:53
  62.8 15.9 %collective-permute-start.19 = (bf16[4,96,512]{2,1,0:T(8,128)(2,1)S(1)}, bf16[4,96,512]{2,1,0:T(8,128)(2,1)S(1)}, u32[]{:S(2)}, u32[]{:S(2)}) collective-permute-start(bf16[4,96,512]{2,1,0:T(8,128)(2,1)S(1)} %pad_maximum_fusion.4), channel_id=1, source_target_pairs={{0,8},{1,9},{2,10},{3,11},{4,12},{5,13},{6,14},{7,15},{8,24},{9,25... | collective-permute-start | bytes 1179656 | tf_op jit(solution)/shard_map/ppermute | solution.py:53
  65.1 13.5 %collective-permute-start.20 = (bf16[2,96,512]{2,1,0:T(8,128)(2,1)S(1)}, bf16[2,96,512]{2,1,0:T(8,128)(2,1)S(1)}, u32[]{:S(2)}, u32[]{:S(2)}) collective-permute-start(bf16[2,96,512]{2,1,0:T(8,128)(2,1)S(1)} %slice.34), channel_id=1, source_target_pairs={{0,16},{1,17},{2,18},{3,19},{4,20},{5,21},{6,22},{7,23},{8,0},{9,1... | collective-permute-start | bytes 589832 | tf_op jit(solution)/shard_map/ppermute | solution.py:53
  78.6 3.5 %collective-permute-start.24 = (bf16[8,96,768]{2,1,0:T(8,128)(2,1)S(1)}, bf16[8,96,768]{2,1,0:T(8,128)(2,1)S(1)}, u32[]{:S(2)}, u32[]{:S(2)}) collective-permute-start(bf16[8,96,768]{2,1,0:T(8,128)(2,1)S(1)} %collective-permute-done.18.refs_5_.refs_8_), channel_id=1, source_target_pairs={{0,1},{1,0},{2,3},{3,2},{4,5},{5,4},{6,7},{7,6},{8,9},{9,8},{10,11... | collective-permute-start | bytes 3538952 | tf_op jit(solution)/shard_map/ppermute | solution.py:53
  78.7 10.6 %collective-permute-start.26 = (bf16[4,96,512]{2,1,0:T(8,128)(2,1)S(1)}, bf16[4,96,512]{2,1,0:T(8,128)(2,1)S(1)}, u32[]{:S(2)}, u32[]{:S(2)}) collective-permute-start(bf16[4,96,512]{2,1,0:T(8,128)(2,1)S(1)} %collective-permute-done.19.refs_12_), channel_id=1, source_target_pairs={{0,1},{1,0},{2,3},{3,2},{4,5},{5,4},{6,7},{7,6},{8,9},{9,8},{10,11... | collective-permute-start | bytes 1179656 | tf_op jit(solution)/shard_map/ppermute | solution.py:53
  79.3 8.5 %collective-permute-start.21 = (bf16[2,96,512]{2,1,0:T(8,128)(2,1)S(1)}, bf16[2,96,512]{2,1,0:T(8,128)(2,1)S(1)}, u32[]{:S(2)}, u32[]{:S(2)}) collective-permute-start(bf16[2,96,512]{2,1,0:T(8,128)(2,1)S(1)} %slice.37), channel_id=1, source_target_pairs={{0,8},{1,9},{2,10},{3,11},{4,12},{5,13},{6,14},{7,15},{8,24},{9,25... | collective-permute-start | bytes 589832 | tf_op jit(solution)/shard_map/ppermute | solution.py:53
  80.9 7.8 %collective-permute-start.22 = (bf16[8,96,256]{2,1,0:T(8,128)(2,1)S(1)}, bf16[8,96,256]{2,1,0:T(8,128)(2,1)S(1)}, u32[]{:S(2)}, u32[]{:S(2)}) collective-permute-start(bf16[8,96,256]{2,1,0:T(8,128)(2,1)S(1)} %slice.38), channel_id=1, source_target_pairs={{0,2},{1,5},{2,0},{3,7},{4,6},{5,1},{6,4},{7,3},{8,10},{9,13},{10,... | collective-permute-start | bytes 1179656 | tf_op jit(solution)/shard_map/ppermute | solution.py:53
  82.1 7.2 %collective-permute-start.25 = (bf16[4,96,512]{2,1,0:T(8,128)(2,1)S(1)}, bf16[4,96,512]{2,1,0:T(8,128)(2,1)S(1)}, u32[]{:S(2)}, u32[]{:S(2)}) collective-permute-start(bf16[4,96,512]{2,1,0:T(8,128)(2,1)S(1)} %collective-permute-done.17.refs_10_), channel_id=1, source_target_pairs={{0,1},{1,0},{2,3},{3,2},{4,5},{5,4},{6,7},{7,6},{8,9},{9,8},{10,11... | collective-permute-start | bytes 1179656 | tf_op jit(solution)/shard_map/ppermute | solution.py:53
  82.2 7.2 %collective-permute-start.27 = (bf16[2,96,512]{2,1,0:T(8,128)(2,1)S(1)}, bf16[2,96,512]{2,1,0:T(8,128)(2,1)S(1)}, u32[]{:S(2)}, u32[]{:S(2)}) collective-permute-start(bf16[2,96,512]{2,1,0:T(8,128)(2,1)S(1)} %collective-permute-done.20.refs_14_), channel_id=1, source_target_pairs={{0,1},{1,0},{2,3},{3,2},{4,5},{5,4},{6,7},{7,6},{8,9},{9,8},{10,11... | collective-permute-start | bytes 589832 | tf_op jit(solution)/shard_map/ppermute | solution.py:53
  88.7 1.4 %collective-permute-start.28 = (bf16[2,96,512]{2,1,0:T(8,128)(2,1)S(1)}, bf16[2,96,512]{2,1,0:T(8,128)(2,1)S(1)}, u32[]{:S(2)}, u32[]{:S(2)}) collective-permute-start(bf16[2,96,512]{2,1,0:T(8,128)(2,1)S(1)} %collective-permute-done.21.refs_16_), channel_id=1, source_target_pairs={{0,1},{1,0},{2,3},{3,2},{4,5},{5,4},{6,7},{7,6},{8,9},{9,8},{10,11... | collective-permute-start | bytes 589832 | tf_op jit(solution)/shard_map/ppermute | solution.py:53
  88.8 6.5 %collective-permute-start.29 = (bf16[8,96,256]{2,1,0:T(8,128)(2,1)S(1)}, bf16[8,96,256]{2,1,0:T(8,128)(2,1)S(1)}, u32[]{:S(2)}, u32[]{:S(2)}) collective-permute-start(bf16[8,96,256]{2,1,0:T(8,128)(2,1)S(1)} %collective-permute-done.22.refs_10_), channel_id=1, source_target_pairs={{0,1},{1,0},{2,3},{3,2},{4,5},{5,4},{6,7},{7,6},{8,9},{9,8},{10,11... | collective-permute-start | bytes 1179656 | tf_op jit(solution)/shard_map/ppermute | solution.py:53
  95.2 5.2 %copy-start.3 = (f32[1,768]{1,0:T(1,128)S(1)}, f32[1,768]{1,0:T(1,128)}, u32[]{:S(2)}) copy-start(f32[1,768]{1,0:T(1,128)} %copy-done.2) | copy-start | bytes 9220
  100.4 13.0 %copy-start.18 = (f32[768]{0:T(1024)S(1)}, f32[768]{0:T(1024)}, u32[]{:S(2)}) copy-start(f32[768]{0:T(1024)} %param.30) | copy-start | bytes 9220
  100.5 17.7 %copy-start.6 = (s32[8]{0:T(128)S(1)}, s32[8]{0:T(128)}, u32[]{:S(2)}) copy-start(s32[8]{0:T(128)} %refs_1_.3) | copy-start | bytes 100
  113.2 1.3 collective-permute-start.30
  114.6 7.3 %collective-permute-start.31 = (bf16[100,384]{1,0:T(8,128)(2,1)S(1)}, bf16[100,384]{1,0:T(8,128)(2,1)S(1)}, u32[]{:S(2)}, u32[]{:S(2)}) collective-permute-start(bf16[100,384]{1,0:T(8,128)(2,1)S(1)} %shard_map.183.refs_0_), channel_id=1, source_target_pairs={{0,4},{1,5},{2,6},{3,7},{4,0},{5,1},{6,2},{7,3},{8,12},{9,13},{10,... | collective-permute-start | bytes 230408 | tf_op jit(solution)/shard_map/ppermute | solution.py:53
  115.5 6.4 %collective-permute-start.32 = (bf16[100,384]{1,0:T(8,128)(2,1)S(1)}, bf16[100,384]{1,0:T(8,128)(2,1)S(1)}, u32[]{:S(2)}, u32[]{:S(2)}) collective-permute-start(bf16[100,384]{1,0:T(8,128)(2,1)S(1)} %shard_map.183.refs_0_), channel_id=1, source_target_pairs={{0,2},{1,3},{2,0},{3,1},{4,6},{5,7},{6,4},{7,5},{8,10},{9,11},{10,... | collective-permute-start | bytes 230408 | tf_op jit(solution)/shard_map/ppermute | solution.py:53
  117.1 5.3 %collective-permute-start.33 = (bf16[100,384]{1,0:T(8,128)(2,1)S(1)}, bf16[100,384]{1,0:T(8,128)(2,1)S(1)}, u32[]{:S(2)}, u32[]{:S(2)}) collective-permute-start(bf16[100,384]{1,0:T(8,128)(2,1)S(1)} %shard_map.183.refs_0_), channel_id=1, source_target_pairs={{0,6},{1,7},{2,4},{3,5},{4,2},{5,3},{6,0},{7,1},{8,14},{9,15},{10,... | collective-permute-start | bytes 230408 | tf_op jit(solution)/shard_map/ppermute | solution.py:53
  122.5 4.5 %collective-permute-start.34 = (bf16[100,384]{1,0:T(8,128)(2,1)S(1)}, bf16[100,384]{1,0:T(8,128)(2,1)S(1)}, u32[]{:S(2)}, u32[]{:S(2)}) collective-permute-start(bf16[100,384]{1,0:T(8,128)(2,1)S(1)} %shard_map.184.refs_0_), channel_id=1, source_target_pairs={{0,8},{1,9},{2,10},{3,11},{4,12},{5,13},{6,14},{7,15},{8,0},{9,1},... | collective-permute-start | bytes 230408 | tf_op jit(solution)/shard_map/ppermute | solution.py:53
  127.0 5.4 %collective-permute-start.35 = (bf16[100,384]{1,0:T(8,128)(2,1)S(1)}, bf16[100,384]{1,0:T(8,128)(2,1)S(1)}, u32[]{:S(2)}, u32[]{:S(2)}) collective-permute-start(bf16[100,384]{1,0:T(8,128)(2,1)S(1)} %shard_map.185.refs_0_), channel_id=1, source_target_pairs={{0,16},{1,17},{2,18},{3,19},{4,20},{5,21},{6,22},{7,23},{8,24},{9,... | collective-permute-start | bytes 230408 | tf_op jit(solution)/shard_map/ppermute | solution.py:53
  132.4 1.3 collective-permute-start.36
  (8 other events, 29.0 us)
where the time goes:
time: 135 us
  Pallas kernels  46.2 us (34%)
  waiting for transfers between devices  40.6 us (30%)
  starting transfers between devices  37.2 us (28%)
  local copies, waits for them, and re-layouts  8.19 us (6%)
    pallas_call x11, Pallas kernels, call(): pl.pallas_call(skip, in_specs=[SMEM] * len(scalars) + [VMEM] * len(operan...  43.5 us
    ppermute x37, waiting for transfers between devices, move(): return lax.ppermute(value, BOTH, device_perm(self.count, target))  40.6 us
    ppermute x37, starting transfers between devices, move(): return lax.ppermute(value, BOTH, device_perm(self.count, target))  37.2 us
    reshape x2, local copies, waits for them, and re-layouts, per_device(): result.reshape(result.shape[0], images, width)  3.94 us
  transfers between devices with their start and end apart: 37, of which 18 were waited for; matrix products, arithmetic and copies ran while one was open for 4% of the time, Pallas kernels for 19%

commit v1 on v0

--- a/solution.py
+++ b/solution.py
@@ -400,18 +400,28 @@
 def mlp_kernel(loader, chunk, slots, first, *refs):
     place, normed, grad, bias = refs[:4]
     refs = refs[4:]
-    refs = refs if first else refs[2:]
+    sums_in, refs = (None, refs) if first else (refs[:2], refs[2:])
     pieces = refs[: loader.count]
     out_sum, back_sum, up, down = refs[loader.count :]
     loader.run(place, pieces, put_mlp(up, down, chunk, slots))
-    if first:
-        out_sum[...] = jnp.zeros_like(out_sum)
-        back_sum[...] = jnp.zeros_like(back_sum)
     half = normed.shape[0] // 2
     step = 1024
-
-    @pl.loop(0, up.shape[1] // step)
-    def _(index):
+    for start in range(0, up.shape[1], step):
+        cols = slice(start, start + step)
+        for part in range(2):
+            rows = slice(part * half, (part + 1) * half)
+            pre = dot(normed[rows], up[:, cols], NN) + bias[:, cols]
+            grad_active = dot(grad[rows], down[:, cols], NN)
+            chance, density = gelu_parts(pre)
+            active = (pre * chance).astype(BF16)
+            grad_pre = (grad_active * (chance + pre * density)).astype(BF16)
+            made = dot(active, down[:, cols], NT), dot(grad_pre, up[:, cols], NT)
+            held = sums_in if start == 0 else (out_sum, back_sum)
+            for index, (total, value) in enumerate(zip((out_sum, back_sum), made)):
+                total[rows] = value if held is None else held[index][rows] + value
+
+
+def _(index):
         cols = lanes_at(index * step, step)
         for part in range(2):
             rows = slice(part * half, (part + 1) * half)

time: 135 us -> 135 us (level)
  no operation moved by 1% of the time
where the time goes in v1:
time: 135 us
  Pallas kernels  46.6 us (35%)
  waiting for transfers between devices  40.6 us (30%)
  starting transfers between devices  37.1 us (27%)
  local copies, waits for them, and re-layouts  8.19 us (6%)
    pallas_call x11, Pallas kernels, call(): pl.pallas_call(skip, in_specs=[SMEM] * len(scalars) + [VMEM] * len(operan...  44 us
    ppermute x37, waiting for transfers between devices, move(): return lax.ppermute(value, BOTH, device_perm(self.count, target))  40.6 us
    ppermute x37, starting transfers between devices, move(): return lax.ppermute(value, BOTH, device_perm(self.count, target))  37.1 us
    reshape x2, local copies, waits for them, and re-layouts, per_device(): result.reshape(result.shape[0], images, width)  3.94 us
  transfers between devices with their start and end apart: 37, of which 18 were waited for; matrix products, arithmetic and copies ran while one was open for 4% of the time, Pallas kernels for 19%

profile of v1, /device:TPU:0, one launch (start us, length us, event | category | flops | bytes accessed | tf_op | source)
XLA Modules:
  0.0 135.0 jit_solution(2926712472710370845)
XLA Ops:
  1.3 2.6 %shard_map.175 = (bf16[96,768]{1,0:T(8,128)(2,1)}, bf16[96,1280]{1,0:T(8,128)(2,1)}, bf16[96,1024]{1,0:T(8,128)(2,1)}) custom-call(s32[5]{0:T(128)} %stack.37.place.refs_0_, bf16[3,96,192]{2,1,0:T(8,128)(2,1)} %w_qkv.1, bf16[192,96]{1,0:T(8,128)(2,1)} %w_out.1, bf16[96,768]{1,0:T(8,128)(2,1)} %w_fc1.1, bf16[96,768]{1,0:T(8,128)(2,1)} %bitcast.33), custom_call_target="tpu_custom_call" | custom-call | flops 100000000 | bytes 100000000 | tf_op jit(solution)/shard_map/pallas_call | solution.py:577
  3.9 3.1 %collective-permute-start.2 = (bf16[1,96,768]{2,1,0:T(8,128)(2,1)}, bf16[1,96,768]{2,1,0:T(8,128)(2,1)S(1)}, u32[]{:S(2)}, u32[]{:S(2)}) collective-permute-start(bf16[1,96,768]{2,1,0:T(8,128)(2,1)} %bitcast.34), channel_id=1, source_target_pairs={{0,8},{1,9},{2,10},{3,11},{4,12},{5,13},{6,14},{7,15},{8,24},{9,25... | collective-permute-start | bytes 442376 | tf_op jit(solution)/shard_map/ppermute | solution.py:53
  7.0 1.1 collective-permute-start.1
  8.1 1.8 %collective-permute-start = (bf16[1,96,1280]{2,1,0:T(8,128)(2,1)}, bf16[1,96,1280]{2,1,0:T(8,128)(2,1)S(1)}, u32[]{:S(2)}, u32[]{:S(2)}) collective-permute-start(bf16[1,96,1280]{2,1,0:T(8,128)(2,1)} %bitcast.28), channel_id=1, source_target_pairs={{0,4},{1,3},{2,6},{3,1},{4,0},{5,7},{6,2},{7,5},{8,12},{9,11},{10,... | collective-permute-start | bytes 737288 | tf_op jit(solution)/shard_map/ppermute | solution.py:53
  9.9 2.3 %collective-permute-done.2 = bf16[1,96,768]{2,1,0:T(8,128)(2,1)S(1)} collective-permute-done((bf16[1,96,768]{2,1,0:T(8,128)(2,1)}, bf16[1,96,768]{2,1,0:T(8,128)(2,1)S(1)}, u32[]{:S(2)}, u32[]{:S(2)}) %collective-permute-start.2) | collective-permute-done | bytes 147488 | tf_op jit(solution)/shard_map/ppermute | solution.py:53
  12.2 3.1 %collective-permute-done.1 = bf16[1,96,768]{2,1,0:T(8,128)(2,1)S(1)} collective-permute-done((bf16[1,96,768]{2,1,0:T(8,128)(2,1)}, bf16[1,96,768]{2,1,0:T(8,128)(2,1)S(1)}, u32[]{:S(2)}, u32[]{:S(2)}) %collective-permute-start.1) | collective-permute-done | bytes 147488 | tf_op jit(solution)/shard_map/ppermute | solution.py:53
  15.3 1.0 constant_dynamic-update-slice_fusion.1
  16.4 1.6 %collective-permute-start.3 = (bf16[2,96,1280]{2,1,0:T(8,128)(2,1)S(1)}, bf16[2,96,1280]{2,1,0:T(8,128)(2,1)S(1)}, u32[]{:S(2)}, u32[]{:S(2)}) collective-permute-start(bf16[2,96,1280]{2,1,0:T(8,128)(2,1)S(1)} %constant_dynamic-update-slice_fusion.refs_7_.refs_6_), channel_id=1, source_target_pairs={{0,2},{1,5},{2,0},{3,7},{4,6},{5,1},{6,4},{7,3},{8,10},{9,13},{10,... | collective-permute-start | bytes 1474568 | tf_op jit(solution)/shard_map/ppermute | solution.py:53
  18.0 0.7 slice.30
  18.7 1.7 %collective-permute-start.4 = (bf16[1,96,768]{2,1,0:T(8,128)(2,1)}, bf16[1,96,768]{2,1,0:T(8,128)(2,1)S(1)}, u32[]{:S(2)}, u32[]{:S(2)}) collective-permute-start(bf16[1,96,768]{2,1,0:T(8,128)(2,1)} %slice.30), channel_id=1, source_target_pairs={{0,16},{1,17},{2,18},{3,19},{4,20},{5,21},{6,22},{7,23},{8,0},{9,1... | collective-permute-start | bytes 442376 | tf_op jit(solution)/shard_map/ppermute | solution.py:53
  21.2 1.6 %shard_map.176 = (bf16[608,768]{1,0:T(8,128)(2,1)S(1)}, bf16[608,768]{1,0:T(8,128)(2,1)S(1)}, bf16[608,768]{1,0:T(8,128)(2,1)S(1)}, f32[2,1,384]{2,1,0:T(1,128)S(1)}) custom-call(s32[5]{0:T(128)S(1)} %copy-done.4, s32[8]{0:T(128)S(1)} %copy-done.5, bf16[2,197,768]{2,1,0:T(8,128)(2,1)S(1)} %copy.23.refs_2_, bf16[100,768]{1,0:T(8,128)(2,1)S(1)} %copy-done, ...), custom_call_target="tpu_custom_call" | custom-call | flops 100000000 | bytes 100000000 | tf_op jit(solution)/shard_map/pallas_call | solution.py:553
  22.8 1.0 copy-done.7
  24.4 0.9 collective-permute-done.3.refs_8_.refs_7_
  25.3 1.5 %collective-permute-start.6 = (bf16[3,96,768]{2,1,0:T(8,128)(2,1)S(1)}, bf16[3,96,768]{2,1,0:T(8,128)(2,1)S(1)}, u32[]{:S(2)}, u32[]{:S(2)}) collective-permute-start(bf16[3,96,768]{2,1,0:T(8,128)(2,1)S(1)} %pad_maximum_fusion.3), channel_id=1, source_target_pairs={{0,4},{1,3},{2,6},{3,1},{4,0},{5,7},{6,2},{7,5},{8,12},{9,11},{10,... | collective-permute-start | bytes 1327112 | tf_op jit(solution)/shard_map/ppermute | solution.py:53
  27.3 1.7 %collective-permute-start.7 = (bf16[1,96,1024]{2,1,0:T(8,128)(2,1)S(1)}, bf16[1,96,1024]{2,1,0:T(8,128)(2,1)S(1)}, u32[]{:S(2)}, u32[]{:S(2)}) collective-permute-start(bf16[1,96,1024]{2,1,0:T(8,128)(2,1)S(1)} %bitcast.30), channel_id=1, source_target_pairs={{0,16},{1,17},{2,18},{3,19},{4,20},{5,21},{6,22},{7,23},{8,0},{9,1... | collective-permute-start | bytes 589832 | tf_op jit(solution)/shard_map/ppermute | solution.py:53
  29.0 4.6 %collective-permute-done.6 = bf16[3,96,768]{2,1,0:T(8,128)(2,1)S(1)} collective-permute-done((bf16[3,96,768]{2,1,0:T(8,128)(2,1)S(1)}, bf16[3,96,768]{2,1,0:T(8,128)(2,1)S(1)}, u32[]{:S(2)}, u32[]{:S(2)}) %collective-permute-start.6) | collective-permute-done | bytes 442400 | tf_op jit(solution)/shard_map/ppermute | solution.py:53
  34.1 1.5 %collective-permute-start.11 = (bf16[6,96,768]{2,1,0:T(8,128)(2,1)S(1)}, bf16[6,96,768]{2,1,0:T(8,128)(2,1)S(1)}, u32[]{:S(2)}, u32[]{:S(2)}) collective-permute-start(bf16[6,96,768]{2,1,0:T(8,128)(2,1)S(1)} %pad_maximum_fusion.1.refs_11_), channel_id=1, source_target_pairs={{0,2},{1,5},{2,0},{3,7},{4,6},{5,1},{6,4},{7,3},{8,10},{9,13},{10,... | collective-permute-start | bytes 2654216 | tf_op jit(solution)/shard_map/ppermute | solution.py:53
  35.7 2.6 %collective-permute-start.13 = (bf16[1,96,1024]{2,1,0:T(8,128)(2,1)S(1)}, bf16[1,96,1024]{2,1,0:T(8,128)(2,1)S(1)}, u32[]{:S(2)}, u32[]{:S(2)}) collective-permute-start(bf16[1,96,1024]{2,1,0:T(8,128)(2,1)S(1)} %collective-permute-done.7), channel_id=1, source_target_pairs={{0,16},{1,17},{2,18},{3,19},{4,20},{5,21},{6,22},{7,23},{8,0},{9,1... | collective-permute-start | bytes 589832 | tf_op jit(solution)/shard_map/ppermute | solution.py:53
  38.9 8.4 %collective-permute-done.14 = f32[2,768]{1,0:T(2,128)S(1)} collective-permute-done((f32[2,768]{1,0:T(2,128)S(1)}, f32[2,768]{1,0:T(2,128)S(1)}, u32[]{:S(2)}, u32[]{:S(2)}) %collective-permute-start.14) | collective-permute-done | bytes 6176 | tf_op jit(solution)/shard_map/ppermute | solution.py:53
  47.7 1.5 %collective-permute-start.16 = (bf16[4,96,1024]{2,1,0:T(8,128)(2,1)S(1)}, bf16[4,96,1024]{2,1,0:T(8,128)(2,1)S(1)}, u32[]{:S(2)}, u32[]{:S(2)}) collective-permute-start(bf16[4,96,1024]{2,1,0:T(8,128)(2,1)S(1)} %pad_maximum_fusion.2), channel_id=1, source_target_pairs={{0,4},{1,3},{2,6},{3,1},{4,0},{5,7},{6,2},{7,5},{8,12},{9,11},{10,... | collective-permute-start | bytes 2359304 | tf_op jit(solution)/shard_map/ppermute | solution.py:53
  49.7 1.5 %collective-permute-start.17 = (bf16[4,96,512]{2,1,0:T(8,128)(2,1)S(1)}, bf16[4,96,512]{2,1,0:T(8,128)(2,1)S(1)}, u32[]{:S(2)}, u32[]{:S(2)}) collective-permute-start(bf16[4,96,512]{2,1,0:T(8,128)(2,1)S(1)} %pad_maximum_fusion.4), channel_id=1, source_target_pairs={{0,16},{1,17},{2,18},{3,19},{4,20},{5,21},{6,22},{7,23},{8,0},{9,1... | collective-permute-start | bytes 1179656 | tf_op jit(solution)/shard_map/ppermute | solution.py:53
  51.2 8.5 %collective-permute-done.16 = bf16[4,96,1024]{2,1,0:T(8,128)(2,1)S(1)} collective-permute-done((bf16[4,96,1024]{2,1,0:T(8,128)(2,1)S(1)}, bf16[4,96,1024]{2,1,0:T(8,128)(2,1)S(1)}, u32[]{:S(2)}, u32[]{:S(2)}) %collective-permute-start.16) | collective-permute-done | bytes 786464 | tf_op jit(solution)/shard_map/ppermute | solution.py:53
  59.9 0.8 collective-permute-done.17.refs_10_
  60.9 1.9 %collective-permute-start.18 = (bf16[8,96,768]{2,1,0:T(8,128)(2,1)S(1)}, bf16[8,96,768]{2,1,0:T(8,128)(2,1)S(1)}, u32[]{:S(2)}, u32[]{:S(2)}) collective-permute-start(bf16[8,96,768]{2,1,0:T(8,128)(2,1)S(1)} %slice.33), channel_id=1, source_target_pairs={{0,2},{1,5},{2,0},{3,7},{4,6},{5,1},{6,4},{7,3},{8,10},{9,13},{10,... | collective-permute-start | bytes 3538952 | tf_op jit(solution)/shard_map/ppermute | solution.py:53
  62.8 2.3 %collective-permute-start.19 = (bf16[4,96,512]{2,1,0:T(8,128)(2,1)S(1)}, bf16[4,96,512]{2,1,0:T(8,128)(2,1)S(1)}, u32[]{:S(2)}, u32[]{:S(2)}) collective-permute-start(bf16[4,96,512]{2,1,0:T(8,128)(2,1)S(1)} %pad_maximum_fusion.4), channel_id=1, source_target_pairs={{0,8},{1,9},{2,10},{3,11},{4,12},{5,13},{6,14},{7,15},{8,24},{9,25... | collective-permute-start | bytes 1179656 | tf_op jit(solution)/shard_map/ppermute | solution.py:53
  65.1 0.7 collective-permute-start.20
  65.8 10.1 %shard_map.177 = (bf16[3,2,2,384,384]{4,3,2,1,0:T(8,128)(2,1)S(1)}, bf16[3,2,2,304,768]{4,3,2,1,0:T(8,128)(2,1)S(1)}, bf16[3,608,256]{2,1,0:T(8,128)(2,1)S(1)}, ...) custom-call(s32[5]{0:T(128)S(1)} %copy-done.4, ...), custom_call_target="tpu_custom_call" | custom-call | flops 80000000000 | bytes 100000000 | tf_op jit(solution)/shard_map/pallas_call | solution.py:553
  75.8 2.8 %collective-permute-done.20.refs_14_ = bf16[2,96,512]{2,1,0:T(8,128)(2,1)S(1)} collective-permute-done((bf16[2,96,512]{2,1,0:T(8,128)(2,1)S(1)}, bf16[2,96,512]{2,1,0:T(8,128)(2,1)S(1)}, u32[]{:S(2)}, u32[]{:S(2)}) %collective-permute-start.20) | collective-permute-done | bytes 196640 | tf_op jit(solution)/shard_map/ppermute | solution.py:53
  79.3 1.6 %collective-permute-start.21 = (bf16[2,96,512]{2,1,0:T(8,128)(2,1)S(1)}, bf16[2,96,512]{2,1,0:T(8,128)(2,1)S(1)}, u32[]{:S(2)}, u32[]{:S(2)}) collective-permute-start(bf16[2,96,512]{2,1,0:T(8,128)(2,1)S(1)} %slice.37), channel_id=1, source_target_pairs={{0,8},{1,9},{2,10},{3,11},{4,12},{5,13},{6,14},{7,15},{8,24},{9,25... | collective-permute-start | bytes 589832 | tf_op jit(solution)/shard_map/ppermute | solution.py:53
  80.9 1.2 collective-permute-start.22
  82.7 5.1 %shard_map.178 = (f32[608,768]{1,0:T(8,128)S(1)}, f32[608,768]{1,0:T(8,128)S(1)}) custom-call(s32[5]{0:T(128)S(1)} %copy-done.4, bf16[608,768]{1,0:T(8,128)(2,1)S(1)} %get-tuple-element.106.refs_1_, bf16[608,768]{1,0:T(8,128)(2,1)S(1)} %get-tuple-element.107.refs_2_.refs_3_, f32[1,1024]{1,0:T(1,128)S(1)} %bitcast.25, ...), custom_call_target="tpu_custom_call" | custom-call | flops 38252052480 | bytes 160000000 | tf_op jit(solution)/shard_map/pallas_call | solution.py:553
  87.8 0.9 collective-permute-done.22.refs_10_
  89.3 0.8 collective-permute-done.28.refs_17_
  90.2 5.3 %shard_map.179 = (f32[608,768]{1,0:T(8,128)S(1)}, f32[608,768]{1,0:T(8,128)S(1)}) custom-call(s32[5]{0:T(128)S(1)} %copy-done.4, bf16[608,768]{1,0:T(8,128)(2,1)S(1)} %get-tuple-element.106.refs_1_, bf16[608,768]{1,0:T(8,128)(2,1)S(1)} %get-tuple-element.107.refs_2_.refs_3_, f32[1,1024]{1,0:T(1,128)S(1)} %bitcast.24, ...), custom_call_target="tpu_custom_call", output_to_operand_aliasing={{0}: (4, {}), {1}: (5, {})} | custom-call | flops 38252052480 | bytes 160000000 | tf_op jit(solution)/shard_map/pallas_call | solution.py:553
  95.5 5.6 %shard_map.180 = (f32[608,768]{1,0:T(8,128)S(1)}, f32[608,768]{1,0:T(8,128)S(1)}) custom-call(s32[5]{0:T(128)S(1)} %copy-done.4, bf16[608,768]{1,0:T(8,128)(2,1)S(1)} %get-tuple-element.106.refs_1_, bf16[608,768]{1,0:T(8,128)(2,1)S(1)} %get-tuple-element.107.refs_2_.refs_3_, f32[1,1024]{1,0:T(1,128)S(1)} %bitcast.23, ...), custom_call_target="tpu_custom_call", output_to_operand_aliasing={{0}: (4, {}), {1}: (5, {})} | custom-call | flops 38252052480 | bytes 160000000 | tf_op jit(solution)/shard_map/pallas_call | solution.py:553
  101.2 12.5 %shard_map.181 = (f32[100,384]{1,0:T(8,128)S(1)}, bf16[100,384]{1,0:T(8,128)(2,1)S(1)}, f32[2,5,768]{2,1,0:T(8,128)S(1)}, f32[608,768]{1,0:T(8,128)S(1)}, bf16[608,2304]{1,0:T(8,128)(2,1)S(1)}) custom-call(s32[5]{0:T(128)S(1)} %copy-done.4, f32[608,768]{1,0:T(8,128)S(1)} %get-tuple-element.99.refs_1_.refs_2_, f32[608,768]{1,0:T(8,128)S(1)} %get-tuple-element.122.refs_2_, ...), custom_call_target="tpu_custom_call" | custom-call | flops 89999998976 | bytes 240000000 | tf_op jit(solution)/shard_map/pallas_call | solution.py:553
  113.9 1.1 collective-permute-done.30.refs_1_
  115.0 0.9 collective-permute-start.31
  115.9 1.7 %collective-permute-start.32 = (bf16[100,384]{1,0:T(8,128)(2,1)S(1)}, bf16[100,384]{1,0:T(8,128)(2,1)S(1)}, u32[]{:S(2)}, u32[]{:S(2)}) collective-permute-start(bf16[100,384]{1,0:T(8,128)(2,1)S(1)} %shard_map.183.refs_0_), channel_id=1, source_target_pairs={{0,2},{1,3},{2,0},{3,1},{4,6},{5,7},{6,4},{7,5},{8,10},{9,11},{10,... | collective-permute-start | bytes 230408 | tf_op jit(solution)/shard_map/ppermute | solution.py:53
  117.6 0.9 collective-permute-start.33
  118.6 3.8 %shard_map.182 = (bf16[297,1536]{1,0:T(8,128)(2,1)S(1)}, bf16[197,1536]{1,0:T(8,128)(2,1)S(1)}) custom-call(s32[5]{0:T(128)S(1)} %copy-done.4, s32[8]{0:T(128)S(1)} %copy-done.6, f32[608,768]{1,0:T(8,128)S(1)} %get-tuple-element.99.refs_1_.refs_2_, f32[608,768]{1,0:T(8,128)S(1)} %get-tuple-element.120.refs_3_, ...), custom_call_target="tpu_custom_call" | custom-call | flops 20000000000 | bytes 100000000 | tf_op jit(solution)/shard_map/pallas_call | solution.py:553
  123.0 1.4 %collective-permute-start.34 = (bf16[100,384]{1,0:T(8,128)(2,1)S(1)}, bf16[100,384]{1,0:T(8,128)(2,1)S(1)}, u32[]{:S(2)}, u32[]{:S(2)}) collective-permute-start(bf16[100,384]{1,0:T(8,128)(2,1)S(1)} %shard_map.184.refs_0_), channel_id=1, source_target_pairs={{0,8},{1,9},{2,10},{3,11},{4,12},{5,13},{6,14},{7,15},{8,0},{9,1},... | collective-permute-start | bytes 230408 | tf_op jit(solution)/shard_map/ppermute | solution.py:53
  124.4 3.1 %collective-permute-done.34.refs_1_ = bf16[100,384]{1,0:T(8,128)(2,1)S(1)} collective-permute-done((bf16[100,384]{1,0:T(8,128)(2,1)S(1)}, bf16[100,384]{1,0:T(8,128)(2,1)S(1)}, u32[]{:S(2)}, u32[]{:S(2)}) %collective-permute-start.34) | collective-permute-done | bytes 76832 | tf_op jit(solution)/shard_map/ppermute | solution.py:53
  127.5 1.3 collective-permute-start.35
  128.8 2.2 %reshape.51 = bf16[297,2,768]{2,1,0:T(2,128)(2,1)} reshape(bf16[297,1536]{1,0:T(8,128)(2,1)S(1)} %get-tuple-element.131.refs_4_) | data formatting | bytes 1824768 | tf_op jit(solution)/shard_map/reshape | solution.py:797
  131.1 1.7 %reshape.52 = bf16[197,2,768]{2,1,0:T(2,128)(2,1)} reshape(bf16[197,1536]{1,0:T(8,128)(2,1)S(1)} %get-tuple-element.132.refs_5_) | data formatting | bytes 1210368 | tf_op jit(solution)/shard_map/reshape | solution.py:797
  133.0 1.2 collective-permute-done.36
  134.3 0.7 maximum_select_fusion
  (113 shorter events, 8.0 us)
Async XLA Ops:
  0.6 19.8 %copy-start.9 = (bf16[2,297,768]{2,0,1:T(2,128)(2,1)S(1)}, bf16[2,297,768]{2,0,1:T(2,128)(2,1)}, u32[]{:S(2)}) copy-start(bf16[2,297,768]{2,0,1:T(2,128)(2,1)} %param.31) | copy-start | bytes 2737156
  3.9 16.4 %copy-start.10 = (bf16[2,197,768]{2,0,1:T(2,128)(2,1)S(1)}, bf16[2,197,768]{2,0,1:T(2,128)(2,1)}, u32[]{:S(2)}) copy-start(bf16[2,197,768]{2,0,1:T(2,128)(2,1)} %param.16) | copy-start | bytes 1815556
  3.9 8.3 %collective-permute-start.2 = (bf16[1,96,768]{2,1,0:T(8,128)(2,1)}, bf16[1,96,768]{2,1,0:T(8,128)(2,1)S(1)}, u32[]{:S(2)}, u32[]{:S(2)}) collective-permute-start(bf16[1,96,768]{2,1,0:T(8,128)(2,1)} %bitcast.34), channel_id=1, source_target_pairs={{0,8},{1,9},{2,10},{3,11},{4,12},{5,13},{6,14},{7,15},{8,24},{9,25... | collective-permute-start | bytes 442376 | tf_op jit(solution)/shard_map/ppermute | solution.py:53
  7.0 8.2 %collective-permute-start.1 = (bf16[1,96,768]{2,1,0:T(8,128)(2,1)}, bf16[1,96,768]{2,1,0:T(8,128)(2,1)S(1)}, u32[]{:S(2)}, u32[]{:S(2)}) collective-permute-start(bf16[1,96,768]{2,1,0:T(8,128)(2,1)} %bitcast.35), channel_id=1, source_target_pairs={{0,16},{1,17},{2,18},{3,19},{4,20},{5,21},{6,22},{7,23},{8,0},{9,1... | collective-permute-start | bytes 442376 | tf_op jit(solution)/shard_map/ppermute | solution.py:53
  8.1 7.2 %collective-permute-start = (bf16[1,96,1280]{2,1,0:T(8,128)(2,1)}, bf16[1,96,1280]{2,1,0:T(8,128)(2,1)S(1)}, u32[]{:S(2)}, u32[]{:S(2)}) collective-permute-start(bf16[1,96,1280]{2,1,0:T(8,128)(2,1)} %bitcast.28), channel_id=1, source_target_pairs={{0,4},{1,3},{2,6},{3,1},{4,0},{5,7},{6,2},{7,5},{8,12},{9,11},{10,... | collective-permute-start | bytes 737288 | tf_op jit(solution)/shard_map/ppermute | solution.py:53
  16.3 4.9 %copy-start = (bf16[100,768]{1,0:T(8,128)(2,1)S(1)}, bf16[100,768]{1,0:T(8,128)(2,1)}, u32[]{:S(2)}) copy-start(bf16[100,768]{1,0:T(8,128)(2,1)} %refs_3_.1) | copy-start | bytes 460804
  16.4 8.9 %collective-permute-start.3 = (bf16[2,96,1280]{2,1,0:T(8,128)(2,1)S(1)}, bf16[2,96,1280]{2,1,0:T(8,128)(2,1)S(1)}, u32[]{:S(2)}, u32[]{:S(2)}) collective-permute-start(bf16[2,96,1280]{2,1,0:T(8,128)(2,1)S(1)} %constant_dynamic-update-slice_fusion.refs_7_.refs_6_), channel_id=1, source_target_pairs={{0,2},{1,5},{2,0},{3,7},{4,6},{5,1},{6,4},{7,3},{8,10},{9,13},{10,... | collective-permute-start | bytes 1474568 | tf_op jit(solution)/shard_map/ppermute | solution.py:53
  18.7 5.7 %collective-permute-start.4 = (bf16[1,96,768]{2,1,0:T(8,128)(2,1)}, bf16[1,96,768]{2,1,0:T(8,128)(2,1)S(1)}, u32[]{:S(2)}, u32[]{:S(2)}) collective-permute-start(bf16[1,96,768]{2,1,0:T(8,128)(2,1)} %slice.30), channel_id=1, source_target_pairs={{0,16},{1,17},{2,18},{3,19},{4,20},{5,21},{6,22},{7,23},{8,0},{9,1... | collective-permute-start | bytes 442376 | tf_op jit(solution)/shard_map/ppermute | solution.py:53
  20.4 6.9 %copy-start.11 = (bf16[96,1024]{1,0:T(8,128)(2,1)S(1)}, bf16[96,1024]{1,0:T(8,128)(2,1)}, u32[]{:S(2)}) copy-start(bf16[96,1024]{1,0:T(8,128)(2,1)} %get-tuple-element.71) | copy-start | bytes 589828
  20.6 3.1 %collective-permute-start.5 = (f32[768]{0:T(1024)S(1)}, f32[768]{0:T(1024)S(1)}, u32[]{:S(2)}, u32[]{:S(2)}) collective-permute-start(f32[768]{0:T(1024)S(1)} %copy-done.14), channel_id=1, source_target_pairs={{0,1},{1,0},{2,3},{3,2},{4,5},{5,4},{6,7},{7,6},{8,9},{9,8},{10,11... | collective-permute-start | bytes 9224 | tf_op jit(solution)/shard_map/ppermute | solution.py:53
  25.3 8.3 %collective-permute-start.6 = (bf16[3,96,768]{2,1,0:T(8,128)(2,1)S(1)}, bf16[3,96,768]{2,1,0:T(8,128)(2,1)S(1)}, u32[]{:S(2)}, u32[]{:S(2)}) collective-permute-start(bf16[3,96,768]{2,1,0:T(8,128)(2,1)S(1)} %pad_maximum_fusion.3), channel_id=1, source_target_pairs={{0,4},{1,3},{2,6},{3,1},{4,0},{5,7},{6,2},{7,5},{8,12},{9,11},{10,... | collective-permute-start | bytes 1327112 | tf_op jit(solution)/shard_map/ppermute | solution.py:53
  26.8 7.3 %collective-permute-start.8 = (bf16[2,96,1280]{2,1,0:T(8,128)(2,1)S(1)}, bf16[2,96,1280]{2,1,0:T(8,128)(2,1)S(1)}, u32[]{:S(2)}, u32[]{:S(2)}) collective-permute-start(bf16[2,96,1280]{2,1,0:T(8,128)(2,1)S(1)} %constant_dynamic-update-slice_fusion.refs_7_.refs_6_), channel_id=1, source_target_pairs={{0,1},{1,0},{2,3},{3,2},{4,5},{5,4},{6,7},{7,6},{8,9},{9,8},{10,11... | collective-permute-start | bytes 1474568 | tf_op jit(solution)/shard_map/ppermute | solution.py:53
  26.8 7.3 %collective-permute-start.9 = (bf16[2,96,1280]{2,1,0:T(8,128)(2,1)S(1)}, bf16[2,96,1280]{2,1,0:T(8,128)(2,1)S(1)}, u32[]{:S(2)}, u32[]{:S(2)}) collective-permute-start(bf16[2,96,1280]{2,1,0:T(8,128)(2,1)S(1)} %collective-permute-done.3.refs_8_.refs_7_), channel_id=1, source_target_pairs={{0,1},{1,0},{2,3},{3,2},{4,5},{5,4},{6,7},{7,6},{8,9},{9,8},{10,11... | collective-permute-start | bytes 1474568 | tf_op jit(solution)/shard_map/ppermute | solution.py:53
  27.3 6.8 %collective-permute-start.7 = (bf16[1,96,1024]{2,1,0:T(8,128)(2,1)S(1)}, bf16[1,96,1024]{2,1,0:T(8,128)(2,1)S(1)}, u32[]{:S(2)}, u32[]{:S(2)}) collective-permute-start(bf16[1,96,1024]{2,1,0:T(8,128)(2,1)S(1)} %bitcast.30), channel_id=1, source_target_pairs={{0,16},{1,17},{2,18},{3,19},{4,20},{5,21},{6,22},{7,23},{8,0},{9,1... | collective-permute-start | bytes 589832 | tf_op jit(solution)/shard_map/ppermute | solution.py:53
  33.7 17.5 %copy-start.15 = (f32[768]{0:T(1024)S(1)}, f32[768]{0:T(1024)}, u32[]{:S(2)}) copy-start(f32[768]{0:T(1024)} %param.24) | copy-start | bytes 9220
  33.7 17.5 %copy-start.16 = (f32[768]{0:T(1024)S(1)}, f32[768]{0:T(1024)}, u32[]{:S(2)}) copy-start(f32[768]{0:T(1024)} %param.25) | copy-start | bytes 9220
  33.7 17.5 %copy-start.17 = (f32[768]{0:T(1024)S(1)}, f32[768]{0:T(1024)}, u32[]{:S(2)}) copy-start(f32[768]{0:T(1024)} %param.26) | copy-start | bytes 9220
  34.1 13.5 %collective-permute-start.11 = (bf16[6,96,768]{2,1,0:T(8,128)(2,1)S(1)}, bf16[6,96,768]{2,1,0:T(8,128)(2,1)S(1)}, u32[]{:S(2)}, u32[]{:S(2)}) collective-permute-start(bf16[6,96,768]{2,1,0:T(8,128)(2,1)S(1)} %pad_maximum_fusion.1.refs_11_), channel_id=1, source_target_pairs={{0,2},{1,5},{2,0},{3,7},{4,6},{5,1},{6,4},{7,3},{8,10},{9,13},{10,... | collective-permute-start | bytes 2654216 | tf_op jit(solution)/shard_map/ppermute | solution.py:53
  35.7 11.7 %collective-permute-start.13 = (bf16[1,96,1024]{2,1,0:T(8,128)(2,1)S(1)}, bf16[1,96,1024]{2,1,0:T(8,128)(2,1)S(1)}, u32[]{:S(2)}, u32[]{:S(2)}) collective-permute-start(bf16[1,96,1024]{2,1,0:T(8,128)(2,1)S(1)} %collective-permute-done.7), channel_id=1, source_target_pairs={{0,16},{1,17},{2,18},{3,19},{4,20},{5,21},{6,22},{7,23},{8,0},{9,1... | collective-permute-start | bytes 589832 | tf_op jit(solution)/shard_map/ppermute | solution.py:53
  38.2 9.3 %collective-permute-start.12 = (bf16[1,96,1024]{2,1,0:T(8,128)(2,1)S(1)}, bf16[1,96,1024]{2,1,0:T(8,128)(2,1)S(1)}, u32[]{:S(2)}, u32[]{:S(2)}) collective-permute-start(bf16[1,96,1024]{2,1,0:T(8,128)(2,1)S(1)} %bitcast.31), channel_id=1, source_target_pairs={{0,8},{1,9},{2,10},{3,11},{4,12},{5,13},{6,14},{7,15},{8,24},{9,25... | collective-permute-start | bytes 589832 | tf_op jit(solution)/shard_map/ppermute | solution.py:53
  38.5 8.8 %collective-permute-start.14 = (f32[2,768]{1,0:T(2,128)S(1)}, f32[2,768]{1,0:T(2,128)S(1)}, u32[]{:S(2)}, u32[]{:S(2)}) collective-permute-start(f32[2,768]{1,0:T(2,128)S(1)} %maximum_select_fusion.1), channel_id=1, source_target_pairs={{0,2},{1,3},{2,0},{3,1},{4,6},{5,7},{6,4},{7,5},{8,10},{9,11},{10,... | collective-permute-start | bytes 18440 | tf_op jit(solution)/shard_map/ppermute | solution.py:53
  47.7 12.1 %collective-permute-start.16 = (bf16[4,96,1024]{2,1,0:T(8,128)(2,1)S(1)}, bf16[4,96,1024]{2,1,0:T(8,128)(2,1)S(1)}, u32[]{:S(2)}, u32[]{:S(2)}) collective-permute-start(bf16[4,96,1024]{2,1,0:T(8,128)(2,1)S(1)} %pad_maximum_fusion.2), channel_id=1, source_target_pairs={{0,4},{1,3},{2,6},{3,1},{4,0},{5,7},{6,2},{7,5},{8,12},{9,11},{10,... | collective-permute-start | bytes 2359304 | tf_op jit(solution)/shard_map/ppermute | solution.py:53
  49.2 15.9 %collective-permute-start.10 = (bf16[6,96,768]{2,1,0:T(8,128)(2,1)S(1)}, bf16[6,96,768]{2,1,0:T(8,128)(2,1)S(1)}, u32[]{:S(2)}, u32[]{:S(2)}) collective-permute-start(bf16[6,96,768]{2,1,0:T(8,128)(2,1)S(1)} %pad_maximum_fusion.1.refs_11_), channel_id=1, source_target_pairs={{0,1},{1,0},{2,3},{3,2},{4,5},{5,4},{6,7},{7,6},{8,9},{9,8},{10,11... | collective-permute-start | bytes 2654216 | tf_op jit(solution)/shard_map/ppermute | solution.py:53
  49.2 16.6 %collective-permute-start.15 = (bf16[6,96,768]{2,1,0:T(8,128)(2,1)S(1)}, bf16[6,96,768]{2,1,0:T(8,128)(2,1)S(1)}, u32[]{:S(2)}, u32[]{:S(2)}) collective-permute-start(bf16[6,96,768]{2,1,0:T(8,128)(2,1)S(1)} %collective-permute-done.11.refs_13_), channel_id=1, source_target_pairs={{0,1},{1,0},{2,3},{3,2},{4,5},{5,4},{6,7},{7,6},{8,9},{9,8},{10,11... | collective-permute-start | bytes 2654216 | tf_op jit(solution)/shard_map/ppermute | solution.py:53
  49.7 11.0 %collective-permute-start.17 = (bf16[4,96,512]{2,1,0:T(8,128)(2,1)S(1)}, bf16[4,96,512]{2,1,0:T(8,128)(2,1)S(1)}, u32[]{:S(2)}, u32[]{:S(2)}) collective-permute-start(bf16[4,96,512]{2,1,0:T(8,128)(2,1)S(1)} %pad_maximum_fusion.4), channel_id=1, source_target_pairs={{0,16},{1,17},{2,18},{3,19},{4,20},{5,21},{6,22},{7,23},{8,0},{9,1... | collective-permute-start | bytes 1179656 | tf_op jit(solution)/shard_map/ppermute | solution.py:53
  59.9 5.9 %copy-start.8 = (bf16[608,768]{1,0:T(8,128)(2,1)S(1)}, bf16[608,768]{1,0:T(8,128)(2,1)}, u32[]{:S(2)}) copy-start(bf16[608,768]{1,0:T(8,128)(2,1)} %copy-done.7) | copy-start | bytes 2801668
  60.8 21.3 %collective-permute-start.23 = (bf16[8,96,1024]{2,1,0:T(8,128)(2,1)S(1)}, bf16[8,96,1024]{2,1,0:T(8,128)(2,1)S(1)}, u32[]{:S(2)}, u32[]{:S(2)}) collective-permute-start(bf16[8,96,1024]{2,1,0:T(8,128)(2,1)S(1)} %pad_maximum_fusion.refs_4_.refs_6_), channel_id=1, source_target_pairs={{0,1},{1,0},{2,3},{3,2},{4,5},{5,4},{6,7},{7,6},{8,9},{9,8},{10,11... | collective-permute-start | bytes 4718600 | tf_op jit(solution)/shard_map/ppermute | solution.py:53
  60.9 17.7 %collective-permute-start.18 = (bf16[8,96,768]{2,1,0:T(8,128)(2,1)S(1)}, bf16[8,96,768]{2,1,0:T(8,128)(2,1)S(1)}, u32[]{:S(2)}, u32[]{:S(2)}) collective-permute-start(bf16[8,96,768]{2,1,0:T(8,128)(2,1)S(1)} %slice.33), channel_id=1, source_target_pairs={{0,2},{1,5},{2,0},{3,7},{4,6},{5,1},{6,4},{7,3},{8,10},{9,13},{10,... | collective-permute-start | bytes 3538952 | tf_op jit(solution)/shard_map/ppermute | solution.py:53
  62.8 15.9 %collective-permute-start.19 = (bf16[4,96,512]{2,1,0:T(8,128)(2,1)S(1)}, bf16[4,96,512]{2,1,0:T(8,128)(2,1)S(1)}, u32[]{:S(2)}, u32[]{:S(2)}) collective-permute-start(bf16[4,96,512]{2,1,0:T(8,128)(2,1)S(1)} %pad_maximum_fusion.4), channel_id=1, source_target_pairs={{0,8},{1,9},{2,10},{3,11},{4,12},{5,13},{6,14},{7,15},{8,24},{9,25... | collective-permute-start | bytes 1179656 | tf_op jit(solution)/shard_map/ppermute | solution.py:53
  65.1 13.5 %collective-permute-start.20 = (bf16[2,96,512]{2,1,0:T(8,128)(2,1)S(1)}, bf16[2,96,512]{2,1,0:T(8,128)(2,1)S(1)}, u32[]{:S(2)}, u32[]{:S(2)}) collective-permute-start(bf16[2,96,512]{2,1,0:T(8,128)(2,1)S(1)} %slice.34), channel_id=1, source_target_pairs={{0,16},{1,17},{2,18},{3,19},{4,20},{5,21},{6,22},{7,23},{8,0},{9,1... | collective-permute-start | bytes 589832 | tf_op jit(solution)/shard_map/ppermute | solution.py:53
  78.6 3.5 %collective-permute-start.24 = (bf16[8,96,768]{2,1,0:T(8,128)(2,1)S(1)}, bf16[8,96,768]{2,1,0:T(8,128)(2,1)S(1)}, u32[]{:S(2)}, u32[]{:S(2)}) collective-permute-start(bf16[8,96,768]{2,1,0:T(8,128)(2,1)S(1)} %collective-permute-done.18.refs_5_.refs_8_), channel_id=1, source_target_pairs={{0,1},{1,0},{2,3},{3,2},{4,5},{5,4},{6,7},{7,6},{8,9},{9,8},{10,11... | collective-permute-start | bytes 3538952 | tf_op jit(solution)/shard_map/ppermute | solution.py:53
  78.7 10.6 %collective-permute-start.26 = (bf16[4,96,512]{2,1,0:T(8,128)(2,1)S(1)}, bf16[4,96,512]{2,1,0:T(8,128)(2,1)S(1)}, u32[]{:S(2)}, u32[]{:S(2)}) collective-permute-start(bf16[4,96,512]{2,1,0:T(8,128)(2,1)S(1)} %collective-permute-done.19.refs_12_), channel_id=1, source_target_pairs={{0,1},{1,0},{2,3},{3,2},{4,5},{5,4},{6,7},{7,6},{8,9},{9,8},{10,11... | collective-permute-start | bytes 1179656 | tf_op jit(solution)/shard_map/ppermute | solution.py:53
  79.3 8.5 %collective-permute-start.21 = (bf16[2,96,512]{2,1,0:T(8,128)(2,1)S(1)}, bf16[2,96,512]{2,1,0:T(8,128)(2,1)S(1)}, u32[]{:S(2)}, u32[]{:S(2)}) collective-permute-start(bf16[2,96,512]{2,1,0:T(8,128)(2,1)S(1)} %slice.37), channel_id=1, source_target_pairs={{0,8},{1,9},{2,10},{3,11},{4,12},{5,13},{6,14},{7,15},{8,24},{9,25... | collective-permute-start | bytes 589832 | tf_op jit(solution)/shard_map/ppermute | solution.py:53
  80.9 7.8 %collective-permute-start.22 = (bf16[8,96,256]{2,1,0:T(8,128)(2,1)S(1)}, bf16[8,96,256]{2,1,0:T(8,128)(2,1)S(1)}, u32[]{:S(2)}, u32[]{:S(2)}) collective-permute-start(bf16[8,96,256]{2,1,0:T(8,128)(2,1)S(1)} %slice.38), channel_id=1, source_target_pairs={{0,2},{1,5},{2,0},{3,7},{4,6},{5,1},{6,4},{7,3},{8,10},{9,13},{10,... | collective-permute-start | bytes 1179656 | tf_op jit(solution)/shard_map/ppermute | solution.py:53
  82.1 7.2 %collective-permute-start.25 = (bf16[4,96,512]{2,1,0:T(8,128)(2,1)S(1)}, bf16[4,96,512]{2,1,0:T(8,128)(2,1)S(1)}, u32[]{:S(2)}, u32[]{:S(2)}) collective-permute-start(bf16[4,96,512]{2,1,0:T(8,128)(2,1)S(1)} %collective-permute-done.17.refs_10_), channel_id=1, source_target_pairs={{0,1},{1,0},{2,3},{3,2},{4,5},{5,4},{6,7},{7,6},{8,9},{9,8},{10,11... | collective-permute-start | bytes 1179656 | tf_op jit(solution)/shard_map/ppermute | solution.py:53
  82.2 7.2 %collective-permute-start.27 = (bf16[2,96,512]{2,1,0:T(8,128)(2,1)S(1)}, bf16[2,96,512]{2,1,0:T(8,128)(2,1)S(1)}, u32[]{:S(2)}, u32[]{:S(2)}) collective-permute-start(bf16[2,96,512]{2,1,0:T(8,128)(2,1)S(1)} %collective-permute-done.20.refs_14_), channel_id=1, source_target_pairs={{0,1},{1,0},{2,3},{3,2},{4,5},{5,4},{6,7},{7,6},{8,9},{9,8},{10,11... | collective-permute-start | bytes 589832 | tf_op jit(solution)/shard_map/ppermute | solution.py:53
  88.7 1.4 %collective-permute-start.28 = (bf16[2,96,512]{2,1,0:T(8,128)(2,1)S(1)}, bf16[2,96,512]{2,1,0:T(8,128)(2,1)S(1)}, u32[]{:S(2)}, u32[]{:S(2)}) collective-permute-start(bf16[2,96,512]{2,1,0:T(8,128)(2,1)S(1)} %collective-permute-done.21.refs_16_), channel_id=1, source_target_pairs={{0,1},{1,0},{2,3},{3,2},{4,5},{5,4},{6,7},{7,6},{8,9},{9,8},{10,11... | collective-permute-start | bytes 589832 | tf_op jit(solution)/shard_map/ppermute | solution.py:53
  88.8 6.7 %collective-permute-start.29 = (bf16[8,96,256]{2,1,0:T(8,128)(2,1)S(1)}, bf16[8,96,256]{2,1,0:T(8,128)(2,1)S(1)}, u32[]{:S(2)}, u32[]{:S(2)}) collective-permute-start(bf16[8,96,256]{2,1,0:T(8,128)(2,1)S(1)} %collective-permute-done.22.refs_10_), channel_id=1, source_target_pairs={{0,1},{1,0},{2,3},{3,2},{4,5},{5,4},{6,7},{7,6},{8,9},{9,8},{10,11... | collective-permute-start | bytes 1179656 | tf_op jit(solution)/shard_map/ppermute | solution.py:53
  95.5 5.6 %copy-start.3 = (f32[1,768]{1,0:T(1,128)S(1)}, f32[1,768]{1,0:T(1,128)}, u32[]{:S(2)}) copy-start(f32[1,768]{1,0:T(1,128)} %copy-done.2) | copy-start | bytes 9220
  101.1 12.8 %copy-start.18 = (f32[768]{0:T(1024)S(1)}, f32[768]{0:T(1024)}, u32[]{:S(2)}) copy-start(f32[768]{0:T(1024)} %param.30) | copy-start | bytes 9220
  101.1 17.4 %copy-start.6 = (s32[8]{0:T(128)S(1)}, s32[8]{0:T(128)}, u32[]{:S(2)}) copy-start(s32[8]{0:T(128)} %refs_1_.3) | copy-start | bytes 100
  113.7 1.3 collective-permute-start.30
  115.0 7.3 %collective-permute-start.31 = (bf16[100,384]{1,0:T(8,128)(2,1)S(1)}, bf16[100,384]{1,0:T(8,128)(2,1)S(1)}, u32[]{:S(2)}, u32[]{:S(2)}) collective-permute-start(bf16[100,384]{1,0:T(8,128)(2,1)S(1)} %shard_map.183.refs_0_), channel_id=1, source_target_pairs={{0,4},{1,5},{2,6},{3,7},{4,0},{5,1},{6,2},{7,3},{8,12},{9,13},{10,... | collective-permute-start | bytes 230408 | tf_op jit(solution)/shard_map/ppermute | solution.py:53
  115.9 6.4 %collective-permute-start.32 = (bf16[100,384]{1,0:T(8,128)(2,1)S(1)}, bf16[100,384]{1,0:T(8,128)(2,1)S(1)}, u32[]{:S(2)}, u32[]{:S(2)}) collective-permute-start(bf16[100,384]{1,0:T(8,128)(2,1)S(1)} %shard_map.183.refs_0_), channel_id=1, source_target_pairs={{0,2},{1,3},{2,0},{3,1},{4,6},{5,7},{6,4},{7,5},{8,10},{9,11},{10,... | collective-permute-start | bytes 230408 | tf_op jit(solution)/shard_map/ppermute | solution.py:53
  117.6 5.3 %collective-permute-start.33 = (bf16[100,384]{1,0:T(8,128)(2,1)S(1)}, bf16[100,384]{1,0:T(8,128)(2,1)S(1)}, u32[]{:S(2)}, u32[]{:S(2)}) collective-permute-start(bf16[100,384]{1,0:T(8,128)(2,1)S(1)} %shard_map.183.refs_0_), channel_id=1, source_target_pairs={{0,6},{1,7},{2,4},{3,5},{4,2},{5,3},{6,0},{7,1},{8,14},{9,15},{10,... | collective-permute-start | bytes 230408 | tf_op jit(solution)/shard_map/ppermute | solution.py:53
  123.0 4.5 %collective-permute-start.34 = (bf16[100,384]{1,0:T(8,128)(2,1)S(1)}, bf16[100,384]{1,0:T(8,128)(2,1)S(1)}, u32[]{:S(2)}, u32[]{:S(2)}) collective-permute-start(bf16[100,384]{1,0:T(8,128)(2,1)S(1)} %shard_map.184.refs_0_), channel_id=1, source_target_pairs={{0,8},{1,9},{2,10},{3,11},{4,12},{5,13},{6,14},{7,15},{8,0},{9,1},... | collective-permute-start | bytes 230408 | tf_op jit(solution)/shard_map/ppermute | solution.py:53
  127.5 5.4 %collective-permute-start.35 = (bf16[100,384]{1,0:T(8,128)(2,1)S(1)}, bf16[100,384]{1,0:T(8,128)(2,1)S(1)}, u32[]{:S(2)}, u32[]{:S(2)}) collective-permute-start(bf16[100,384]{1,0:T(8,128)(2,1)S(1)} %shard_map.185.refs_0_), channel_id=1, source_target_pairs={{0,16},{1,17},{2,18},{3,19},{4,20},{5,21},{6,22},{7,23},{8,24},{9,... | collective-permute-start | bytes 230408 | tf_op jit(solution)/shard_map/ppermute | solution.py:53
  132.9 1.3 collective-permute-start.36
  (8 other events, 29.0 us)
